TPU v7x, 512 devices: a whole 4x8x8 slice. The times are simulated.
512 devices in a mesh: seq: 128 (over y, z, core), ch: 4 (over x).
Axes of the slice: x: 4, y: 8, z: 8, core: 2. Of those that a mesh axis runs over, the one named last changes fastest.
Arguments:
- inputs: bfloat16 [1024, 16384], P('ch', 'seq'), may hold values from -6 to 6
- out_grad: bfloat16 [1024, 16384], P('ch', 'seq'), may hold values from -6 to 6
- readout: float32 [2, 1024, 64], P(None, 'ch'), may hold values from -4 to 4
- log_step: float32 [1024], P('ch'), may hold values from -10.5 to -3
- decay_log: float32 [64], replicated, may hold values from -1.4 to 0
- rotation: float32 [64], replicated, may hold values from 0 to 200
Outputs:
- kernel_grad: float32 [1024, 16384], P('ch', 'seq')
- readout_grad: float32 [2, 1024, 64], P(None, 'ch')
- step_grad: float32 [1024], P('ch')
- state_grad: float32 [2, 64], replicated
All inputs are finite; a program needn't handle non-finite values.
Results may differ from a plain program's by a relative error of at most 0.0005.
Values may be sent and summed in bfloat16 or wider, within the bound.
A program may use at most 64 MiB of HBM per device.

v0:
```python
import math

import jax
import jax.numpy as jnp
from jax import lax
from jax.sharding import PartitionSpec as P

precise = lax.Precision.HIGHEST
two_pi = 2.0 * math.pi


def angle_table(left_index, right_index, modulus, orient):
    product = left_index[:, None] * right_index[None, :] % modulus
    return orient * two_pi * product.astype(jnp.float32) / modulus


def rotate(real_part, imag_part, angles):
    cosine_table = jnp.cos(angles)
    sine_table = jnp.sin(angles)
    return (
        real_part * cosine_table - imag_part * sine_table,
        real_part * sine_table + imag_part * cosine_table,
    )


def last_transform(real_part, imag_part, orient):
    length = real_part.shape[-1]
    counter = jnp.arange(length, dtype=jnp.int32)
    angles = angle_table(counter, counter, length, orient)
    cosine_table = jnp.cos(angles)
    sine_table = jnp.sin(angles)
    out_real = jnp.dot(
        real_part, cosine_table, precision=precise, preferred_element_type=jnp.float32
    ) - jnp.dot(imag_part, sine_table, precision=precise, preferred_element_type=jnp.float32)
    out_imag = jnp.dot(
        imag_part, cosine_table, precision=precise, preferred_element_type=jnp.float32
    ) + jnp.dot(real_part, sine_table, precision=precise, preferred_element_type=jnp.float32)
    return (out_real, out_imag)


def correlation_spectrum(in_real, in_imag, out_real, out_imag):
    return (out_real * in_real + out_imag * in_imag, out_imag * in_real - out_real * in_imag)


def discretize(readout, log_step, decay_log, rotation):
    step_size = jnp.exp(log_step)[:, None]
    pole_real = -jnp.exp(decay_log)[None, :]
    pole_imag = rotation[None, :]
    rate_real = step_size * pole_real
    rate_imag = step_size * pole_imag
    lift_real = jnp.expm1(rate_real) * jnp.cos(rate_imag) - 2.0 * jnp.sin(0.5 * rate_imag) ** 2
    lift_imag = jnp.exp(rate_real) * jnp.sin(rate_imag)
    pole_norm = pole_real * pole_real + pole_imag * pole_imag
    ratio_real = (lift_real * pole_real + lift_imag * pole_imag) / pole_norm
    ratio_imag = (lift_imag * pole_real - lift_real * pole_imag) / pole_norm
    coef_real = readout[0] * ratio_real - readout[1] * ratio_imag
    coef_imag = readout[0] * ratio_imag + readout[1] * ratio_real
    return (coef_real, coef_imag, rate_real, rate_imag)


def parameter_grads(primal, backward, totals):
    coef_real, coef_imag = (primal[0], primal[1])
    cotangents = (
        2.0 * totals[0],
        -2.0 * totals[1],
        2.0 * (coef_real * totals[2] - coef_imag * totals[3]),
        -2.0 * (coef_real * totals[3] + coef_imag * totals[2]),
    )
    return backward(cotangents)


def shifted_totals(raw_sums, rate_real, rate_imag, block_start, norm_scale):
    decays = jnp.exp(rate_real * block_start)
    phases = rate_imag * block_start
    base_real = decays * jnp.cos(phases)
    base_imag = decays * jnp.sin(phases)
    near_real = block_start * raw_sums[0] + raw_sums[2]
    near_imag = block_start * raw_sums[1] + raw_sums[3]
    return jnp.stack(
        [
            norm_scale * (base_real * raw_sums[0] - base_imag * raw_sums[1]),
            norm_scale * (base_real * raw_sums[1] + base_imag * raw_sums[0]),
            norm_scale * (base_real * near_real - base_imag * near_imag),
            norm_scale * (base_real * near_imag + base_imag * near_real),
        ]
    )


def power_sums(pieces):
    lag_rows, rate_real, rate_imag = pieces
    length = lag_rows.shape[-1]
    offsets = jnp.arange(length, dtype=jnp.int32).astype(jnp.float32)
    decays = jnp.exp(rate_real[:, :, None] * offsets)
    phases = rate_imag[:, :, None] * offsets
    power_real = decays * jnp.cos(phases)
    power_imag = decays * jnp.sin(phases)
    weighted = lag_rows * offsets
    return jnp.stack(
        [
            jnp.einsum("gj,gnj->gn", lag_rows, power_real, precision=precise),
            jnp.einsum("gj,gnj->gn", lag_rows, power_imag, precision=precise),
            jnp.einsum("gj,gnj->gn", weighted, power_real, precision=precise),
            jnp.einsum("gj,gnj->gn", weighted, power_imag, precision=precise),
        ]
    )


def block_channels(channels, states, length):
    group_size = channels & -channels
    while group_size > 1 and group_size * states * length > 1048576:
        group_size = group_size // 2
    return group_size


def per_device(inputs, out_grad, readout, log_step, decay_log, rotation):
    owners = lax.axis_size("seq")
    self_index = lax.axis_index("seq")
    channels, length = inputs.shape
    states = decay_log.shape[0]
    freq_width = 2 * owners
    modulus = freq_width * length
    norm_scale = 1.0 / math.sqrt(owners * length)
    block_len = length // owners
    stacked = jnp.stack([inputs, out_grad]).reshape(2, channels, owners, block_len)
    signal = lax.all_to_all(stacked, "seq", split_axis=2, concat_axis=2, tiled=True).astype(
        jnp.float32
    )
    source = jnp.arange(owners, dtype=jnp.int32)
    target = jnp.arange(freq_width, dtype=jnp.int32)
    across = angle_table(source, target, freq_width, -1.0)
    across_cos = jnp.cos(across)
    across_sin = jnp.sin(across)
    positions = self_index * block_len + jnp.arange(block_len, dtype=jnp.int32)
    twiddle = angle_table(target, positions, modulus, -1.0)
    lag_index = jnp.arange(length, dtype=jnp.int32)
    spec_real = jnp.einsum("ahdq,dk->ahkq", signal, across_cos, precision=precise)
    spec_imag = jnp.einsum("ahdq,dk->ahkq", signal, across_sin, precision=precise)
    turn_real, turn_imag = rotate(spec_real, spec_imag, twiddle)
    arrived = lax.all_to_all(
        jnp.stack([turn_real, turn_imag]), "seq", split_axis=3, concat_axis=4, tiled=True
    )
    freq_real, freq_imag = last_transform(arrived[0], arrived[1], -1.0)
    prod_real, prod_imag = correlation_spectrum(
        freq_real[0], freq_imag[0], freq_real[1], freq_imag[1]
    )
    back_real, back_imag = last_transform(prod_real, prod_imag, 1.0)
    pair_index = 2 * self_index + jnp.arange(2, dtype=jnp.int32)
    back_real, back_imag = rotate(
        back_real, back_imag, angle_table(pair_index, lag_index, modulus, 1.0)
    )
    outgoing = jnp.stack([back_real, back_imag]).reshape(2, channels, 2, owners, block_len)
    landed = lax.all_to_all(outgoing, "seq", split_axis=3, concat_axis=2, tiled=True).reshape(
        2, channels, freq_width, block_len
    )
    inverse = angle_table(target, source, freq_width, 1.0)
    lag_part = jnp.einsum(
        "hkq,kd->hdq", landed[0], jnp.cos(inverse), precision=precise
    ) - jnp.einsum("hkq,kd->hdq", landed[1], jnp.sin(inverse), precision=precise)
    lag_part = lag_part * (norm_scale / modulus)
    kernel_grad = lax.all_to_all(lag_part, "seq", split_axis=1, concat_axis=2, tiled=True).reshape(
        channels, length
    )
    primal, backward = jax.vjp(discretize, readout, log_step, decay_log, rotation)
    group_size = block_channels(channels, states, length)
    group_count = channels // group_size
    raw_sums = lax.map(
        power_sums,
        (
            kernel_grad.reshape(group_count, group_size, length),
            primal[2].reshape(group_count, group_size, states),
            primal[3].reshape(group_count, group_size, states),
        ),
    )
    raw_sums = jnp.transpose(raw_sums, (1, 0, 2, 3)).reshape(4, channels, states)
    block_start = (self_index * length).astype(jnp.float32)
    partial_totals = shifted_totals(raw_sums, primal[2], primal[3], block_start, norm_scale)
    totals = lax.psum(partial_totals, "seq")
    readout_grad, step_grad, decay_grad, rotation_grad = parameter_grads(primal, backward, totals)
    state_grad = lax.psum(jnp.stack([decay_grad, rotation_grad]), "ch")
    return (kernel_grad, readout_grad, step_grad, state_grad)


def solution(mesh):
    return jax.shard_map(
        per_device,
        mesh=mesh,
        in_specs=(P("ch", "seq"), P("ch", "seq"), P(None, "ch", None), P("ch"), P(), P()),
        out_specs=(P("ch", "seq"), P(None, "ch", None), P("ch"), P()),
        check_vma=False,
    )
```

profile of v0, /device:TPU:1, one launch (start us, length us, event | category | flops | bytes accessed | tf_op | source)
XLA Modules:
  0.0 529.4 jit_solution(17954254751322689666)
XLA Ops:
  7.2 0.9 maximum_bitcast_fusion.2
  8.8 18.4 %all-to-all-start = ((bf16[2,256,128,1]{1,0,3,2:T(2,128)(2,1)}), bf16[2,256,128,1]{1,0,3,2:T(2,128)(2,1)S(1)}, u32[]{:S(2)}, u32[]{:S(2)}) async-start(bf16[2,256,128,1]{1,0,3,2:T(2,128)(2,1)} %copy.38), calls=%async_computation | async-start | bytes 262144 | tf_op jit(solution)/shard_map/all_to_all | solution.py:125
  27.3 12.2 %all-to-all-done = bf16[2,256,128,1]{1,0,3,2:T(2,128)(2,1)S(1)} async-done(((bf16[2,256,128,1]{1,0,3,2:T(2,128)(2,1)}), bf16[2,256,128,1]{1,0,3,2:T(2,128)(2,1)S(1)}, u32[]{:S(2)}, u32[]{:S(2)}) %all-to-all-start) | async-done | bytes 131104 | tf_op jit(solution)/shard_map/all_to_all | solution.py:125
  39.7 0.8 convolution_bitcast_fusion
  40.5 0.9 subtract_bitcast_fusion
  41.5 1.8 copy.40
  43.3 6.2 %all-to-all-start.1 = ((f32[2,2,256,256,1]{2,1,4,0,3:T(2,128)}), f32[2,2,256,256,1]{2,1,4,0,3:T(2,128)S(1)}, u32[]{:S(2)}, u32[]{:S(2)}) async-start(f32[2,2,256,256,1]{2,1,4,0,3:T(2,128)} %copy.40), calls=%async_computation.1 | async-start | bytes 2097152 | tf_op jit(solution)/shard_map/all_to_all | solution.py:139
  49.6 30.4 %all-to-all-done.1 = f32[2,2,256,256,1]{2,1,4,0,3:T(2,128)S(1)} async-done(((f32[2,2,256,256,1]{2,1,4,0,3:T(2,128)}), f32[2,2,256,256,1]{2,1,4,0,3:T(2,128)S(1)}, u32[]{:S(2)}, u32[]{:S(2)}) %all-to-all-start.1) | async-done | bytes 1048608 | tf_op jit(solution)/shard_map/all_to_all | solution.py:139
  80.5 0.8 fusion.25
  81.4 0.8 fusion.26
  82.2 0.8 convolution_subtract_fusion
  83.0 0.8 convolution_add_fusion
  86.5 1.0 copy.43
  87.5 7.0 %all-to-all-start.2 = ((f32[2,256,2,128,1]{1,2,0,4,3:T(2,128)}), f32[2,256,2,128,1]{1,2,0,4,3:T(2,128)S(1)}, u32[]{:S(2)}, u32[]{:S(2)}) async-start(f32[2,256,2,128,1]{1,2,0,4,3:T(2,128)} %copy.43), calls=%async_computation.2 | async-start | bytes 1048576 | tf_op jit(solution)/shard_map/all_to_all | solution.py:152
  94.5 19.5 %all-to-all-done.2 = f32[2,256,2,128,1]{1,2,0,4,3:T(2,128)S(1)} async-done(((f32[2,256,2,128,1]{1,2,0,4,3:T(2,128)}), f32[2,256,2,128,1]{1,2,0,4,3:T(2,128)S(1)}, u32[]{:S(2)}, u32[]{:S(2)}) %all-to-all-start.2) | async-done | bytes 524320 | tf_op jit(solution)/shard_map/all_to_all | solution.py:152
  114.4 0.9 fusion.48
  115.5 0.9 fusion.24
  117.2 7.3 %all-to-all-start.3 = ((f32[256,128,1]{0,2,1:T(1,128)}), f32[256,128,1]{0,2,1:T(1,128)S(1)}, u32[]{:S(2)}, u32[]{:S(2)}) async-start(f32[256,128,1]{0,2,1:T(1,128)} %copy.44), calls=%async_computation.3 | async-start | bytes 262144 | tf_op jit(solution)/shard_map/all_to_all | solution.py:160
  124.7 12.2 %all-to-all-done.3 = f32[256,128,1]{0,2,1:T(1,128)S(1)} async-done(((f32[256,128,1]{0,2,1:T(1,128)}), f32[256,128,1]{0,2,1:T(1,128)S(1)}, u32[]{:S(2)}, u32[]{:S(2)}) %all-to-all-start.3) | async-done | bytes 131104 | tf_op jit(solution)/shard_map/all_to_all | solution.py:160
  136.8 185.6 %while.10 = (s32[]{:T(128)}, f32[2,4,128,64]{3,2,1,0:T(8,128)S(1)}, f32[2,128,128]{1,0,2:T(2,128)S(1)}, f32[2,128,64]{2,1,0:T(8,128)S(1)}, f32[2,128,64]{2,1,0:T(8,128)S(1)}, /*index=5*/s32[]{:T(128)}) while((s32[]{:T(128)}, f32[2,4,128,64]{3,2,1,0:T(8,128)S(1)}, f32[2,128,128]{1,0,2:T(2,128)S(1)}, f32[2,128,64]{2,1,0:T(8,128)S(1)}, ...), condition=%wide.region_1.2_spmd, body=%wide.region_0.1_spmd.sunk | while | flops 63029376 | bytes 1707089 | solution.py:166
  137.1 23.1 %fusion.262 = f32[128,1,64]{2,1,0:T(1,128)S(1)} fusion(f32[128,128,1]{1,2,0:T(1,128)S(1)} %bitcast.255, f32[128,64]{1,0:T(8,128)S(1)} %get-tuple-element.166, f32[128]{0:T(128)S(1)} %iota_convert_fusion.2, f32[128,64]{1,0:T(8,128)S(1)} %get-tuple-element.167), kind=kOutput, calls=%fused_computation.7.clone.1 | convolution fusion | flops 15728640 | bytes 164352 | tf_op jit(solution)/shard_map/while/body/eval_jaxpr/gj,gnj->gn/dot_general | solution.py:102
  160.1 23.2 %fusion.261 = f32[128,1,64]{2,1,0:T(1,128)S(1)} fusion(f32[128,128,1]{1,2,0:T(1,128)S(1)} %bitcast.256, f32[128,64]{1,0:T(8,128)S(1)} %get-tuple-element.166, f32[128]{0:T(128)S(1)} %iota_convert_fusion.2, f32[128,64]{1,0:T(8,128)S(1)} %get-tuple-element.167), kind=kOutput, calls=%fused_computation.5.clone.1 | convolution fusion | flops 15728640 | bytes 164352 | tf_op jit(solution)/shard_map/while/body/eval_jaxpr/gj,gnj->gn/dot_general | solution.py:103
  183.3 23.2 %fusion.263 = f32[128,1,64]{2,1,0:T(1,128)S(1)} fusion(f32[128,128,1]{1,2,0:T(1,128)S(1)} %bitcast.245, f32[128,64]{1,0:T(8,128)S(1)} %get-tuple-element.166, f32[128]{0:T(128)S(1)} %iota_convert_fusion.2, f32[128,64]{1,0:T(8,128)S(1)} %get-tuple-element.167), kind=kOutput, calls=%fused_computation.6.clone.1 | convolution fusion | flops 15728640 | bytes 164352 | tf_op jit(solution)/shard_map/while/body/eval_jaxpr/gj,gnj->gn/dot_general | solution.py:101
  206.5 23.1 %fusion.264 = f32[128,1,64]{2,1,0:T(1,128)S(1)} fusion(f32[128,128,1]{1,2,0:T(1,128)S(1)} %bitcast.246, f32[128,64]{1,0:T(8,128)S(1)} %get-tuple-element.166, f32[128]{0:T(128)S(1)} %iota_convert_fusion.2, f32[128,64]{1,0:T(8,128)S(1)} %get-tuple-element.167), kind=kOutput, calls=%fused_computation.8.clone.1 | convolution fusion | flops 15728640 | bytes 164352 | tf_op jit(solution)/shard_map/while/body/eval_jaxpr/gj,gnj->gn/dot_general | solution.py:100
  229.8 23.1 %fusion.262 = f32[128,1,64]{2,1,0:T(1,128)S(1)} fusion(f32[128,128,1]{1,2,0:T(1,128)S(1)} %bitcast.255, f32[128,64]{1,0:T(8,128)S(1)} %get-tuple-element.166, f32[128]{0:T(128)S(1)} %iota_convert_fusion.2, f32[128,64]{1,0:T(8,128)S(1)} %get-tuple-element.167), kind=kOutput, calls=%fused_computation.7.clone.1 | convolution fusion | flops 15728640 | bytes 164352 | tf_op jit(solution)/shard_map/while/body/eval_jaxpr/gj,gnj->gn/dot_general | solution.py:102
  252.9 23.2 %fusion.261 = f32[128,1,64]{2,1,0:T(1,128)S(1)} fusion(f32[128,128,1]{1,2,0:T(1,128)S(1)} %bitcast.256, f32[128,64]{1,0:T(8,128)S(1)} %get-tuple-element.166, f32[128]{0:T(128)S(1)} %iota_convert_fusion.2, f32[128,64]{1,0:T(8,128)S(1)} %get-tuple-element.167), kind=kOutput, calls=%fused_computation.5.clone.1 | convolution fusion | flops 15728640 | bytes 164352 | tf_op jit(solution)/shard_map/while/body/eval_jaxpr/gj,gnj->gn/dot_general | solution.py:103
  276.1 23.2 %fusion.263 = f32[128,1,64]{2,1,0:T(1,128)S(1)} fusion(f32[128,128,1]{1,2,0:T(1,128)S(1)} %bitcast.245, f32[128,64]{1,0:T(8,128)S(1)} %get-tuple-element.166, f32[128]{0:T(128)S(1)} %iota_convert_fusion.2, f32[128,64]{1,0:T(8,128)S(1)} %get-tuple-element.167), kind=kOutput, calls=%fused_computation.6.clone.1 | convolution fusion | flops 15728640 | bytes 164352 | tf_op jit(solution)/shard_map/while/body/eval_jaxpr/gj,gnj->gn/dot_general | solution.py:101
  299.3 23.1 %fusion.264 = f32[128,1,64]{2,1,0:T(1,128)S(1)} fusion(f32[128,128,1]{1,2,0:T(1,128)S(1)} %bitcast.246, f32[128,64]{1,0:T(8,128)S(1)} %get-tuple-element.166, f32[128]{0:T(128)S(1)} %iota_convert_fusion.2, f32[128,64]{1,0:T(8,128)S(1)} %get-tuple-element.167), kind=kOutput, calls=%fused_computation.8.clone.1 | convolution fusion | flops 15728640 | bytes 164352 | tf_op jit(solution)/shard_map/while/body/eval_jaxpr/gj,gnj->gn/dot_general | solution.py:100
  324.7 183.5 %all-reduce.6.cloned.1.call-done = f32[4,256,64]{1,2,0:T(8,128)} async-done(((f32[4,256,64]{1,2,0:T(8,128)}), f32[4,256,64]{1,2,0:T(8,128)}) %all-reduce.6.cloned.1.call-update) | async-done | bytes 262160 | tf_op jit(solution)/shard_map/psum | solution.py:177
  508.2 1.6 fusion.80
  509.9 1.8 fusion.86
  511.7 9.0 %psum.15 = f32[2,64]{1,0:T(2,128)} all-reduce(f32[2,64]{1,0:T(2,128)S(1)} %pad_maximum_fusion.2), channel_id=1, replica_groups=mesh['seq'=128,'ch'=4] {'ch'}, use_global_device_ids=true, to_apply=%region_13.14 | all-reduce | flops 128 | bytes 1024 | tf_op jit(solution)/shard_map/psum | solution.py:179
  (58 shorter events, 10.4 us)
Async XLA Ops:
  8.8 30.7 %all-to-all-start = ((bf16[2,256,128,1]{1,0,3,2:T(2,128)(2,1)}), bf16[2,256,128,1]{1,0,3,2:T(2,128)(2,1)S(1)}, u32[]{:S(2)}, u32[]{:S(2)}) async-start(bf16[2,256,128,1]{1,0,3,2:T(2,128)(2,1)} %copy.38), calls=%async_computation | async-start | bytes 262144 | tf_op jit(solution)/shard_map/all_to_all | solution.py:125
  43.3 36.7 %all-to-all-start.1 = ((f32[2,2,256,256,1]{2,1,4,0,3:T(2,128)}), f32[2,2,256,256,1]{2,1,4,0,3:T(2,128)S(1)}, u32[]{:S(2)}, u32[]{:S(2)}) async-start(f32[2,2,256,256,1]{2,1,4,0,3:T(2,128)} %copy.40), calls=%async_computation.1 | async-start | bytes 2097152 | tf_op jit(solution)/shard_map/all_to_all | solution.py:139
  86.5 8.0 %copy-start.2 = (f32[64]{0:T(128)S(1)}, f32[64]{0:T(128)}, u32[]{:S(2)}) copy-start(f32[64]{0:T(128)} %param.13) | copy-start | bytes 772
  86.5 8.0 %copy-start.4 = (f32[64]{0:T(128)S(1)}, f32[64]{0:T(128)}, u32[]{:S(2)}) copy-start(f32[64]{0:T(128)} %param.12) | copy-start | bytes 772
  87.5 26.6 %all-to-all-start.2 = ((f32[2,256,2,128,1]{1,2,0,4,3:T(2,128)}), f32[2,256,2,128,1]{1,2,0,4,3:T(2,128)S(1)}, u32[]{:S(2)}, u32[]{:S(2)}) async-start(f32[2,256,2,128,1]{1,2,0,4,3:T(2,128)} %copy.43), calls=%async_computation.2 | async-start | bytes 1048576 | tf_op jit(solution)/shard_map/all_to_all | solution.py:152
  114.4 10.1 %copy-start.3 = (f32[256]{0:T(256)S(1)}, f32[256]{0:T(256)}, u32[]{:S(2)}) copy-start(f32[256]{0:T(256)} %param.11) | copy-start | bytes 3076
  117.2 19.7 %all-to-all-start.3 = ((f32[256,128,1]{0,2,1:T(1,128)}), f32[256,128,1]{0,2,1:T(1,128)S(1)}, u32[]{:S(2)}, u32[]{:S(2)}) async-start(f32[256,128,1]{0,2,1:T(1,128)} %copy.44), calls=%async_computation.3 | async-start | bytes 262144 | tf_op jit(solution)/shard_map/all_to_all | solution.py:160
  124.5 383.8 %all-reduce.6.cloned.1.call-start = ((), (), s32[]{:S(2)}) async-start(), calls=%async_computation.4 | async-start | bytes 524288 | tf_op jit(solution)/shard_map/psum | solution.py:177
  322.5 185.7 %copy-start.1 = (f32[2,256,64]{1,2,0:T(8,128)S(1)}, f32[2,256,64]{1,2,0:T(8,128)}, u32[]{:S(2)}) copy-start(f32[2,256,64]{1,2,0:T(8,128)} %param.10) | copy-start | bytes 393220
  508.2 13.0 %copy-start = (f32[4,256,64]{1,2,0:T(8,128)S(1)}, f32[4,256,64]{1,2,0:T(8,128)}, u32[]{:S(2)}) copy-start(f32[4,256,64]{1,2,0:T(8,128)} %all-reduce.6.cloned.1.call-done) | copy-start | bytes 786436
Sparse Core Ops, SparseCore 0:
  324.1 184.1 all-reduce.5
where the time goes:
time: 533 us; the launch traced here: 529 us
  waiting for transfers between devices  258 us (48%)
  matrix products  194 us (36%)
  starting transfers between devices  38.9 us (7%)
  between operations  14.4 us (3%)
  blocking collectives  8.96 us (2%)
  other arithmetic  7.81 us (1%)
  local copies, waits for them, and re-layouts  7.14 us (1%)
    psum x1, waiting for transfers between devices, per_device(): totals = lax.psum(partial_totals, 'seq')  184 us
    dot_general x2, matrix products, power_sums(): jnp.einsum('gj,gnj->gn', lag_rows, power_imag, precision=precise)  46.4 us
    dot_general x2, matrix products, power_sums(): jnp.einsum('gj,gnj->gn', weighted, power_imag, precision=precise)  46.4 us
    dot_general x2, matrix products, power_sums(): jnp.einsum('gj,gnj->gn', weighted, power_real, precision=precise)  46.1 us
    dot_general x2, matrix products, power_sums(): jnp.einsum('gj,gnj->gn', lag_rows, power_real, precision=precise)  46.1 us
    all_to_all x1, waiting for transfers between devices, per_device(): lax.all_to_all(jnp.stack([turn_real, turn_imag]), 'seq', split_axis=3, co...  30.4 us
    all_to_all x1, waiting for transfers between devices, per_device(): lax.all_to_all(outgoing, 'seq', split_axis=3, concat_axis=2, tiled=True)  19.5 us
    all_to_all x1, starting transfers between devices, per_device(): lax.all_to_all(stacked, 'seq', split_axis=2, concat_axis=2, tiled=True)  18.4 us
  transfers between devices with their start and end apart: 5, of which 5 were waited for; matrix products, arithmetic and copies ran while one was open for 0% of the time, Pallas kernels for 0%

commit v1 on v0

v1 whole, which is shorter than its diff:
```python
import functools
import math

import jax
import jax.numpy as jnp
import numpy as np
from jax import lax
from jax.experimental import pallas as pl
from jax.experimental.pallas import tpu as pltpu
from jax.sharding import PartitionSpec as P

MESH = pl.DeviceIdType.MESH
RINGS = (8, 8, 2)
OWNERS = 128
WIDTH = 128
LENGTH = OWNERS * WIDTH
STATES = 64


def split_table(table):
    whole = jnp.asarray(np.asarray(table, np.float32))
    high = np.asarray(table, np.float32).astype(jnp.bfloat16)
    low = (np.asarray(table, np.float64) - high.astype(np.float64)).astype(jnp.bfloat16)
    del whole
    return np.stack([high, low])


def transform_tables():
    index = np.arange(WIDTH, dtype=np.float64)
    quarter = index + 0.25
    enter = 2.0 * np.pi * np.outer(quarter, index) / WIDTH
    spread = np.zeros((2, 2, WIDTH, OWNERS, 2))
    for channel in range(2):
        spread[0, channel, :, :, channel] = np.cos(enter)
        spread[1, channel, :, :, channel] = -np.sin(enter)
    first = spread.reshape(4 * WIDTH, 2 * OWNERS)
    turn = 2.0 * np.pi * np.outer(quarter, index) / LENGTH
    turns = np.stack([np.cos(turn), np.sin(turn)]).astype(np.float32)
    plain = 2.0 * np.pi * np.outer(index, index) / WIDTH
    cosine, sine = np.cos(plain), np.sin(plain)
    second = np.block([[cosine, -sine], [sine, cosine]])
    third = np.block([[cosine, sine], [-sine, cosine]])
    scale = 1.0 / (LENGTH * math.sqrt(LENGTH))
    leave = enter.T
    fourth = np.concatenate([np.cos(leave), -np.sin(leave)], axis=1) * scale
    return (
        split_table(first),
        turns,
        split_table(second),
        split_table(third),
        split_table(fourth),
    )


def dot(left, right):
    return jnp.dot(left, right, preferred_element_type=jnp.float32)


def halves(value):
    high = value.astype(jnp.bfloat16)
    return high, (value - high.astype(jnp.float32)).astype(jnp.bfloat16)


def dot_pair(left, right):
    return dot(left[0], right[0]) + (dot(left[0], right[1]) + dot(left[1], right[0]))


def sine_cosine(angle):
    turns = jnp.floor(angle * (2.0 / math.pi) + 0.5)
    rest = angle - turns * 1.5625
    rest = rest - turns * 0.0081787109375
    rest = rest - turns * 0.000116348266601562
    rest = rest - turns * 1.26759079665e-06
    square = rest * rest
    sine = rest + rest * square * (
        -1.6666667e-1 + square * (8.3333310e-3 + square * (-1.9840874e-4 + square * 2.7525562e-6))
    )
    cosine = (
        1.0
        - 0.5 * square
        + square
        * square
        * (4.16666667e-2 + square * (-1.38888889e-3 + square * (2.48015873e-5 - square * 2.7557319e-7)))
    )
    quadrant = turns - 4.0 * jnp.floor(turns * 0.25)
    odd = (quadrant == 1.0) | (quadrant == 3.0)
    sine_out = jnp.where(odd, cosine, sine)
    cosine_out = jnp.where(odd, sine, cosine)
    sine_out = jnp.where(quadrant >= 2.0, -sine_out, sine_out)
    cosine_out = jnp.where((quadrant == 1.0) | (quadrant == 2.0), -cosine_out, cosine_out)
    return sine_out, cosine_out


def exp_minus_one(value):
    series = 1.0 + value * (1.0 / 9.0)
    for count in (8.0, 7.0, 6.0, 5.0, 4.0, 3.0, 2.0):
        series = 1.0 + value * (1.0 / count) * series
    return jnp.where(jnp.abs(value) < 0.5, value * series, jnp.exp(value) - 1.0)


def multiply(left, right):
    return (left[0] * right[0] - left[1] * right[1], left[0] * right[1] + left[1] * right[0])


def conjugate(value):
    return (value[0], -value[1])


def primal_rows(step, decay, turn, readout):
    pole = (-jnp.exp(decay), turn)
    rate = (step * pole[0], step * pole[1])
    sine, cosine = sine_cosine(rate[1])
    half_sine, _ = sine_cosine(0.5 * rate[1])
    growth = jnp.exp(rate[0])
    lift = (
        exp_minus_one(rate[0]) * cosine - 2.0 * half_sine * half_sine,
        growth * sine,
    )
    norm = pole[0] * pole[0] + pole[1] * pole[1]
    inverse = (pole[0] / norm, -pole[1] / norm)
    ratio = multiply(lift, inverse)
    coef = multiply(readout, ratio)
    power = (growth * cosine, growth * sine)
    return dict(
        step=step, pole=pole, rate=rate, inverse=inverse, ratio=ratio, coef=coef, power=power
    )


def power_table(rate, positions):
    decays = jnp.exp(rate[0] * positions)
    sine, cosine = sine_cosine(rate[1] * positions)
    return decays * cosine, decays * sine


def correlate(signals, first, turns, second, third, fourth):
    spread = dot(first[0], signals) + dot(first[1], signals)
    turn_cos, turn_sin = turns[0], turns[1]
    blocks = []
    for channel in range(2):
        for signal in range(2):
            columns = slice(signal * WIDTH, (signal + 1) * WIDTH)
            real = spread[channel * WIDTH : (channel + 1) * WIDTH, columns]
            imag = spread[(2 + channel) * WIDTH : (3 + channel) * WIDTH, columns]
            blocks.append(
                jnp.concatenate(
                    [real * turn_cos + imag * turn_sin, imag * turn_cos - real * turn_sin], axis=1
                )
            )
    spectrum = dot_pair(halves(jnp.concatenate(blocks, axis=0)), second)
    products = []
    for channel in range(2):
        entry = spectrum[2 * channel * WIDTH : (2 * channel + 1) * WIDTH]
        exit_ = spectrum[(2 * channel + 1) * WIDTH : (2 * channel + 2) * WIDTH]
        in_real, in_imag = entry[:, :WIDTH], entry[:, WIDTH:]
        out_real, out_imag = exit_[:, :WIDTH], exit_[:, WIDTH:]
        products.append(
            jnp.concatenate(
                [
                    out_real * in_real + out_imag * in_imag,
                    out_imag * in_real - out_real * in_imag,
                ],
                axis=1,
            )
        )
    back = dot_pair(halves(jnp.concatenate(products, axis=0)), third)
    columns = []
    for channel in range(2):
        real = back[channel * WIDTH : (channel + 1) * WIDTH, :WIDTH]
        imag = back[channel * WIDTH : (channel + 1) * WIDTH, WIDTH:]
        columns.append(
            jnp.concatenate(
                [real * turn_cos - imag * turn_sin, real * turn_sin + imag * turn_cos], axis=0
            )
        )
    return dot_pair((fourth[0], fourth[1]), halves(jnp.concatenate(columns, axis=1)))


def sum_rows(value):
    return jnp.sum(value, axis=0, keepdims=True)


def power_sums(lags, near, base, starts, offsets, norm_scale):
    stacked = jnp.concatenate([lags[:, :WIDTH], lags[:, WIDTH:]], axis=0)
    tables = jnp.concatenate(
        [near[0], near[1], offsets * near[0], offsets * near[1]], axis=1
    )
    raw = dot_pair(halves(stacked), halves(tables))
    lane = lax.broadcasted_iota(jnp.int32, (OWNERS, WIDTH), 1)
    picked = [
        jnp.where(
            lane < STATES,
            raw[:OWNERS, part * WIDTH : (part + 1) * WIDTH],
            raw[OWNERS:, part * WIDTH : (part + 1) * WIDTH],
        )
        for part in range(4)
    ]
    plain = (picked[0], picked[1])
    lagged = (starts * picked[0] + picked[2], starts * picked[1] + picked[3])
    powers = multiply(base, plain)
    lag_powers = multiply(base, lagged)
    return (
        (norm_scale * sum_rows(powers[0]), norm_scale * sum_rows(powers[1])),
        (norm_scale * sum_rows(lag_powers[0]), norm_scale * sum_rows(lag_powers[1])),
    )


def parameter_rows(primal, readout, powers, lag_powers):
    coef_grad = (2.0 * powers[0], -2.0 * powers[1])
    readout_grad = multiply(conjugate(primal["ratio"]), coef_grad)
    ratio_grad = multiply(conjugate(readout), coef_grad)
    shifted = multiply(primal["coef"], lag_powers)
    lift_grad = multiply(conjugate(primal["inverse"]), ratio_grad)
    through = multiply(conjugate(primal["power"]), lift_grad)
    rate_grad = (2.0 * shifted[0] + through[0], -2.0 * shifted[1] + through[1])
    direct = multiply(conjugate(primal["ratio"]), lift_grad)
    step, pole = primal["step"], primal["pole"]
    pole_grad = (step * rate_grad[0] - direct[0], step * rate_grad[1] - direct[1])
    step_terms = step * (rate_grad[0] * pole[0] + rate_grad[1] * pole[1])
    return readout_grad, step_terms, (pole_grad[0] * pole[0], pole_grad[1])


def offset_of(place, ring):
    return ring // 2 + (1 - 2 * (place % 2)) * ((place + 1) // 2)


def peer_of(me, count):
    y, z, core = me // 16, (me // 2) % 8, me % 2
    to_y = (y + offset_of(count // 16, 8)) % 8
    to_z = (z + offset_of((count // 2) % 8, 8)) % 8
    to_core = (core + 1 - count % 2) % 2
    return to_y * 16 + to_z * 2 + to_core


def per_peer(me, action):
    def step(count, carry):
        action(peer_of(me, count))
        return carry

    lax.fori_loop(0, OWNERS - 1, step, 0)


def kernel(
    norm_scale,
    inputs_ref,
    grads_ref,
    readout_ref,
    log_step_ref,
    states_ref,
    first_ref,
    turns_ref,
    second_ref,
    third_ref,
    fourth_ref,
    lags_out,
    params_out,
    shared_out,
    outgoing,
    arrived,
    lag_rows,
    param_rows,
    state_rows,
    state_sums,
    state_in,
    first,
    turns,
    second,
    third,
    fourth,
    stage_sem,
    table_sem,
    own_sem,
    send_sem,
    signal_sem,
    lag_sem,
    param_sem,
    state_sem,
    cross_sem,
    cross_send_sem,
):
    me = lax.axis_index("seq")
    row = lax.axis_index("ch")
    stages = [
        pltpu.make_async_copy(inputs_ref, outgoing.at[0], stage_sem.at[0]),
        pltpu.make_async_copy(grads_ref, outgoing.at[1], stage_sem.at[1]),
    ]
    loads = [
        pltpu.make_async_copy(source, target, table_sem.at[place])
        for place, (source, target) in enumerate(
            (
                (first_ref, first),
                (turns_ref, turns),
                (second_ref, second),
                (third_ref, third),
                (fourth_ref, fourth),
            )
        )
    ]
    for copy in stages:
        copy.start()
    for copy in loads:
        copy.start()
    barrier = pltpu.get_barrier_semaphore()

    def greet(peer):
        pl.semaphore_signal(barrier, inc=1, device_id={"seq": peer}, device_id_type=MESH)

    per_peer(me, greet)
    for step in range(1, 4):
        pl.semaphore_signal(
            barrier, inc=1, device_id={"ch": (row + step) % 4}, device_id_type=MESH
        )
    for copy in stages:
        copy.wait()
    pl.semaphore_wait(barrier, OWNERS - 1 + 3)

    def exchange(source, target, send, receive):
        def action(peer):
            pltpu.make_async_remote_copy(
                src_ref=source(peer),
                dst_ref=target,
                send_sem=send,
                recv_sem=receive,
                device_id={"seq": peer},
                device_id_type=MESH,
            ).start()

        per_peer(me, action)

    own = pltpu.make_async_copy(outgoing.at[:, me], arrived.at[:, me], own_sem.at[0])
    own.start()
    exchange(lambda peer: outgoing.at[:, peer], arrived.at[:, me], send_sem.at[0], signal_sem)

    lane_row = lax.broadcasted_iota(jnp.int32, (1, WIDTH), 1)
    step_row = jnp.exp(
        jnp.where(lane_row < STATES, log_step_ref[2 * me], log_step_ref[2 * me + 1])
    )
    decay_row = states_ref[0:1, :]
    turn_row = states_ref[1:2, :]
    readout = (readout_ref[0, pl.ds(me, 1), :], readout_ref[1, pl.ds(me, 1), :])
    primal = primal_rows(step_row, decay_row, turn_row, readout)
    offsets = lax.broadcasted_iota(jnp.int32, (WIDTH, WIDTH), 0).astype(jnp.float32)
    starts = offsets * float(WIDTH)
    near = power_table(primal["rate"], offsets)
    base = power_table(primal["rate"], starts)
    for copy in loads:
        copy.wait()

    own.wait()
    rest = arrived.at[:, pl.ds(0, OWNERS - 1)]
    pltpu.make_async_copy(rest, rest, signal_sem).wait()
    signals = jnp.concatenate(
        [arrived.reshape(2, 2 * OWNERS, WIDTH)[0], arrived.reshape(2, 2 * OWNERS, WIDTH)[1]],
        axis=1,
    )
    lags = correlate(signals, first, turns, second, third, fourth)
    lag_rows[:, 0, :] = lags[:, :WIDTH]
    lag_rows[:, 1, :] = lags[:, WIDTH:]
    own_lags = pltpu.make_async_copy(lag_rows.at[me], lags_out.at[me], own_sem.at[1])
    own_lags.start()
    exchange(lambda peer: lag_rows.at[peer], lags_out.at[me], send_sem.at[1], lag_sem)

    powers, lag_powers = power_sums(lags, near, base, starts, offsets, norm_scale)
    readout_grad, step_terms, state_grad = parameter_rows(primal, readout, powers, lag_powers)
    step_grad = jnp.where(
        lane_row < STATES,
        jnp.sum(jnp.where(lane_row < STATES, step_terms, 0.0), axis=1, keepdims=True),
        jnp.sum(jnp.where(lane_row < STATES, 0.0, step_terms), axis=1, keepdims=True),
    )
    param_rows[0:1, :] = readout_grad[0]
    param_rows[1:2, :] = readout_grad[1]
    param_rows[2:3, :] = step_grad
    param_rows[3:4, :] = jnp.zeros_like(step_grad)
    own_params = pltpu.make_async_copy(param_rows, params_out.at[me], own_sem.at[2])
    own_params.start()
    state_rows[0:1, :] = state_grad[0]
    state_rows[1:2, :] = state_grad[1]
    crossings = [
        pltpu.make_async_remote_copy(
            src_ref=state_rows,
            dst_ref=state_in.at[step - 1],
            send_sem=cross_send_sem.at[step - 1],
            recv_sem=cross_sem.at[step - 1],
            device_id={"ch": (row + step) % 4},
            device_id_type=MESH,
        )
        for step in range(1, 4)
    ]
    for copy in crossings:
        copy.start()
    exchange(lambda peer: param_rows, params_out.at[me], send_sem.at[2], param_sem)
    for copy in crossings:
        copy.wait()
    state_sums[...] = state_rows[...] + state_in[1] + (state_in[0] + state_in[2])
    own_state = pltpu.make_async_copy(state_sums, shared_out.at[me], own_sem.at[3])
    own_state.start()
    exchange(lambda peer: state_sums, shared_out.at[me], send_sem.at[3], state_sem)

    for copy in (own_lags, own_params, own_state):
        copy.wait()
    for buffer, semaphore in (
        (lags_out, lag_sem),
        (params_out, param_sem),
        (shared_out, state_sem),
    ):
        part = buffer.at[pl.ds(0, OWNERS - 1)]
        pltpu.make_async_copy(part, part, semaphore).wait()
    pltpu.make_async_copy(rest, rest, send_sem.at[0]).wait()
    for buffer, place in ((lags_out, 1), (params_out, 2), (shared_out, 3)):
        part = buffer.at[pl.ds(0, OWNERS - 1)]
        pltpu.make_async_copy(part, part, send_sem.at[place]).wait()


def per_device(tables, inputs, out_grad, readout, log_step, decay_log, rotation):
    norm_scale = 1.0 / math.sqrt(LENGTH)
    states = jnp.stack(
        [jnp.concatenate([decay_log, decay_log]), jnp.concatenate([rotation, rotation])]
    )
    dma = pltpu.SemaphoreType.DMA
    any_space = pl.BlockSpec(memory_space=pl.ANY)
    vmem = pl.BlockSpec(memory_space=pltpu.VMEM)
    smem = pl.BlockSpec(memory_space=pltpu.SMEM)
    lags, params, shared = pl.pallas_call(
        functools.partial(kernel, norm_scale),
        out_shape=(
            jax.ShapeDtypeStruct((OWNERS, 2, WIDTH), jnp.float32),
            jax.ShapeDtypeStruct((OWNERS, 4, WIDTH), jnp.float32),
            jax.ShapeDtypeStruct((OWNERS, 2, WIDTH), jnp.float32),
        ),
        in_specs=[any_space, any_space, vmem, smem, vmem] + [any_space] * 5,
        out_specs=(vmem, vmem, vmem),
        scratch_shapes=[
            pltpu.VMEM((2, OWNERS, 2, WIDTH), jnp.bfloat16),
            pltpu.VMEM((2, OWNERS, 2, WIDTH), jnp.bfloat16),
            pltpu.VMEM((OWNERS, 2, WIDTH), jnp.float32),
            pltpu.VMEM((4, WIDTH), jnp.float32),
            pltpu.VMEM((2, WIDTH), jnp.float32),
            pltpu.VMEM((2, WIDTH), jnp.float32),
            pltpu.VMEM((3, 2, WIDTH), jnp.float32),
        ]
        + [pltpu.VMEM(table.shape, table.dtype) for table in tables]
        + [
            dma((2,)),
            dma((5,)),
            dma((4,)),
            dma((4,)),
            dma,
            dma,
            dma,
            dma,
            dma((3,)),
            dma((3,)),
        ],
        compiler_params=pltpu.CompilerParams(collective_id=0, has_side_effects=True),
        name="channel_rows",
    )(
        inputs.reshape(OWNERS, 2, WIDTH),
        out_grad.reshape(OWNERS, 2, WIDTH),
        readout.reshape(2, OWNERS, WIDTH),
        log_step,
        states,
        *[jnp.asarray(table) for table in tables],
    )
    kernel_grad = lags.reshape(2 * OWNERS, WIDTH)
    readout_grad = jnp.transpose(params[:, :2, :], (1, 0, 2)).reshape(2, 2 * OWNERS, STATES)
    step_grad = params[:, 2, :].reshape(2 * OWNERS, STATES)[:, 0]
    state = jnp.sum(shared, axis=0).reshape(2, 2, STATES)
    return kernel_grad, readout_grad, step_grad, state[:, 0] + state[:, 1]


def solution(mesh):
    tables = transform_tables()
    return jax.shard_map(
        functools.partial(per_device, tables),
        mesh=mesh,
        in_specs=(P("ch", "seq"), P("ch", "seq"), P(None, "ch", None), P("ch"), P(), P()),
        out_specs=(P("ch", "seq"), P(None, "ch", None), P("ch"), P()),
        check_vma=False,
    )
```

time: 533 us -> 65.5 us (0.12)
  waiting for transfers between devices: 258 us -> 0 us
  matrix products: 194 us -> 0 us
  Pallas kernels: 0 us -> 56.1 us
  starting transfers between devices: 38.9 us -> 0 us
  between operations: 14.4 us -> 0.72 us
  blocking collectives: 8.96 us -> 0 us
  other arithmetic: 7.81 us -> 2.31 us
    dot_general x20 -> x0, matrix products: 194 us -> none  [the longest x2 46.4 us: power_sums(): jnp.einsum('gj,gnj->gn', lag_rows, power_imag, precision=precise)]
    psum x1 -> x0, waiting for transfers between devices: 184 us -> none  [per_device(): totals = lax.psum(partial_totals, 'seq')]
    all_to_all x4 -> x0, waiting for transfers between devices: 74.3 us -> none  [the longest x1 30.4 us: per_device(): lax.all_to_all(jnp.stack([turn_real, turn_imag]), 'seq', split_axis=3, co...]
    pallas_call x0 -> x1, Pallas kernels: none -> 56.1 us  [per_device(): pl.pallas_call(functools.partial(kernel, norm_scale), out_shape=(jax.Shap...]
    all_to_all x4 -> x0, starting transfers between devices: 38.9 us -> none  [the longest x1 18.4 us: per_device(): lax.all_to_all(stacked, 'seq', split_axis=2, concat_axis=2, tiled=True)]
    psum x1 -> x0, blocking collectives: 8.96 us -> none  [per_device(): state_grad = lax.psum(jnp.stack([decay_grad, rotation_grad]), 'ch')]
  transfers between devices with their start and end apart: 5 -> 0, of which waited for: 5 -> 0; matrix products, arithmetic and copies ran while one was open for 0% -> 0% of each run, Pallas kernels for 0% -> 0%
where the time goes in v1:
time: 65.5 us; the launch traced here: 65.2 us
  Pallas kernels  56.1 us (86%)
  local copies, waits for them, and re-layouts  6.13 us (9%)
  other arithmetic  2.31 us (4%)
  between operations  0.72 us (1%)
    pallas_call x1, Pallas kernels, per_device(): pl.pallas_call(functools.partial(kernel, norm_scale), out_shape=(jax.Shap...  56.1 us
    unnamed x11, local copies, waits for them, and re-layouts  3.24 us
    slice x2, local copies, waits for them, and re-layouts, per_device(): step_grad = params[:, 2, :].reshape(2 * OWNERS, STATES)[:, 0]  1.82 us

profile of v1, /device:TPU:1, one launch (start us, length us, event | category | flops | bytes accessed | tf_op | source)
XLA Modules:
  0.0 65.2 jit_solution(16031396187131780691)
XLA Ops:
  0.6 0.0 copy-start.2
  0.6 0.0 copy-start.3
  0.7 0.6 copy-done.2
  1.3 0.0 copy-done.3
  1.3 0.1 maximum_bitcast_fusion
  1.4 0.6 pad_maximum_fusion.states_ref
  2.0 1.0 %copy.16 = f32[2,256,64]{2,1,0:T(8,128)S(1)} copy(f32[2,256,64]{1,2,0:T(8,128)} %param.13) | data formatting | bytes 262144 | tf_op args[2]
  3.0 0.8 %reshape.29.readout_ref = f32[2,128,128]{2,1,0:T(8,128)} reshape(f32[2,256,64]{2,1,0:T(8,128)S(1)} %copy.16) | data formatting | bytes 262144 | tf_op jit(solution)/shard_map/reshape | solution.py:458
  3.7 56.1 %channel_rows.1 = (f32[128,2,128]{2,1,0:T(2,128)}, f32[128,4,128]{2,1,0:T(4,128)}, f32[128,2,128]{2,1,0:T(2,128)}) custom-call(bf16[128,2,128]{2,1,0:T(2,128)(2,1)} %bitcast.11, bf16[128,2,128]{2,1,0:T(2,128)(2,1)} %bitcast.12, f32[2,128,128]{2,1,0:T(8,128)} %reshape.29.readout_ref, f32[256]{0:T(256)} %log_step_ref.1, f32[2,128]{1,0:T(2,128)} %pad_maximum_fusion.states_ref, ...), custom_call_target="tpu_custom_call" | custom-call | tf_op jit(solution)/shard_map/channel_rows/pallas_call | solution.py:422
  59.8 0.0 copy-start
  59.8 1.1 %reduce_sum.9 = f32[2,128]{1,0:T(2,128)S(1)} reduce(f32[128,2,128]{2,1,0:T(2,128)} %get-tuple-element.9, f32[]{:T(128)} %constant.5.clone.1), dimensions={0}, to_apply=%region_0.0 | reduce | flops 32512 | bytes 132100 | tf_op jit(solution)/shard_map/reduce_sum | solution.py:466
  60.9 0.1 reshape.32
  61.0 0.6 slice_add_fusion
  61.6 1.1 %slice_reduce_fusion.1 = f32[128,128]{1,0:T(8,128)S(1)} fusion(f32[128,4,128]{2,1,0:T(4,128)} %get-tuple-element.8), kind=kLoop, calls=%fused_computation.2 | loop fusion | bytes 131072 | tf_op jit(solution)/shard_map/slice | solution.py:465
  62.7 0.0 copy-done
  62.8 0.1 reshape_squeeze.3
  62.9 0.7 %slice_reduce_fusion = f32[256]{0:T(256)} fusion(f32[256,64]{1,0:T(8,128)S(1)} %reshape_squeeze.3), kind=kLoop, calls=%fused_computation | loop fusion | bytes 2048 | tf_op jit(solution)/shard_map/slice | solution.py:465
  63.6 0.1 reshape.31
  63.7 0.0 copy-start.1
  63.7 0.8 %copy.18 = f32[2,256,64]{1,2,0:T(8,128)} copy(f32[2,256,64]{2,1,0:T(8,128)S(1)} %reshape.31) | data formatting | bytes 262144
  64.5 0.1 copy-done.1
  64.6 0.7 %copy.20 = f32[256,128]{1,0:T(8,128)} copy(f32[256,128]{1,0:T(8,128)S(1)} %bitcast.10) | data formatting | bytes 262144
  (2 shorter events, 0.1 us)
Async XLA Ops:
  0.6 0.7 %copy-start.2 = (f32[64]{0:T(128)S(1)}, f32[64]{0:T(128)}, u32[]{:S(2)}) copy-start(f32[64]{0:T(128)} %param.15) | copy-start | bytes 772
  0.6 0.7 %copy-start.3 = (f32[64]{0:T(128)S(1)}, f32[64]{0:T(128)}, u32[]{:S(2)}) copy-start(f32[64]{0:T(128)} %param.16) | copy-start | bytes 772
  59.8 2.9 %copy-start = (f32[128,4,128]{2,1,0:T(4,128)S(1)}, f32[128,4,128]{2,1,0:T(4,128)}, u32[]{:S(2)}) copy-start(f32[128,4,128]{2,1,0:T(4,128)} %get-tuple-element.8) | copy-start | bytes 786436
  63.7 0.9 %copy-start.1 = (f32[128,2,128]{2,1,0:T(2,128)S(1)}, f32[128,2,128]{2,1,0:T(2,128)}, u32[]{:S(2)}) copy-start(f32[128,2,128]{2,1,0:T(2,128)} %get-tuple-element.7) | copy-start | bytes 393220

commit v2 on v1

--- a/solution.py
+++ b/solution.py
@@ -10,7 +10,6 @@
 from jax.sharding import PartitionSpec as P
 
 MESH = pl.DeviceIdType.MESH
-RINGS = (8, 8, 2)
 OWNERS = 128
 WIDTH = 128
 LENGTH = OWNERS * WIDTH
@@ -18,10 +17,8 @@
 
 
 def split_table(table):
-    whole = jnp.asarray(np.asarray(table, np.float32))
     high = np.asarray(table, np.float32).astype(jnp.bfloat16)
     low = (np.asarray(table, np.float64) - high.astype(np.float64)).astype(jnp.bfloat16)
-    del whole
     return np.stack([high, low])
 
 
@@ -179,12 +176,9 @@
     return jnp.sum(value, axis=0, keepdims=True)
 
 
-def power_sums(lags, near, base, starts, offsets, norm_scale):
+def power_sums(lags, tables, base, starts, norm_scale):
     stacked = jnp.concatenate([lags[:, :WIDTH], lags[:, WIDTH:]], axis=0)
-    tables = jnp.concatenate(
-        [near[0], near[1], offsets * near[0], offsets * near[1]], axis=1
-    )
-    raw = dot_pair(halves(stacked), halves(tables))
+    raw = dot_pair(halves(stacked), tables)
     lane = lax.broadcasted_iota(jnp.int32, (OWNERS, WIDTH), 1)
     picked = [
         jnp.where(
@@ -223,20 +217,22 @@
     return ring // 2 + (1 - 2 * (place % 2)) * ((place + 1) // 2)
 
 
-def peer_of(me, count):
-    y, z, core = me // 16, (me // 2) % 8, me % 2
-    to_y = (y + offset_of(count // 16, 8)) % 8
-    to_z = (z + offset_of((count // 2) % 8, 8)) % 8
-    to_core = (core + 1 - count % 2) % 2
-    return to_y * 16 + to_z * 2 + to_core
+def place_of(me):
+    return me // 16, (me // 2) % 8, me % 2
+
+
+def ring_places(place, ring):
+    return [(place + offset_of(count, ring)) % ring for count in range(ring)]
 
 
 def per_peer(me, action):
-    def step(count, carry):
-        action(peer_of(me, count))
-        return carry
-
-    lax.fori_loop(0, OWNERS - 1, step, 0)
+    y, z, core = place_of(me)
+    to_y = [16 * other for other in ring_places(y, 8)]
+    to_z = [2 * other for other in ring_places(z, 8)]
+    to_core = [1 - core, core]
+    peers = [at_y + at_z + at_core for at_y in to_y for at_z in to_z for at_core in to_core]
+    for peer in peers[:-1]:
+        action(peer)
 
 
 def kernel(
@@ -245,22 +241,27 @@
     grads_ref,
     readout_ref,
     log_step_ref,
-    states_ref,
+    decay_ref,
+    rotation_ref,
     first_ref,
     turns_ref,
     second_ref,
     third_ref,
     fourth_ref,
     lags_out,
-    params_out,
-    shared_out,
+    readout_out,
+    sums_out,
     outgoing,
     arrived,
     lag_rows,
-    param_rows,
-    state_rows,
-    state_sums,
-    state_in,
+    readout_rows,
+    readout_turned,
+    cross_rows,
+    cross_in,
+    line_rows,
+    line_in,
+    column_rows,
+    column_in,
     first,
     turns,
     second,
@@ -272,13 +273,23 @@
     send_sem,
     signal_sem,
     lag_sem,
-    param_sem,
-    state_sem,
+    readout_sem,
     cross_sem,
-    cross_send_sem,
+    line_sem,
+    column_sem,
 ):
     me = lax.axis_index("seq")
     row = lax.axis_index("ch")
+    y, z, core = place_of(me)
+    barrier = pltpu.get_barrier_semaphore()
+
+    def greet(peer):
+        pl.semaphore_signal(barrier, inc=1, device_id={"seq": peer}, device_id_type=MESH)
+
+    per_peer(me, greet)
+    rows_across = [(row + step) % 4 for step in range(1, 4)]
+    for other in rows_across:
+        pl.semaphore_signal(barrier, inc=1, device_id={"ch": other}, device_id_type=MESH)
     stages = [
         pltpu.make_async_copy(inputs_ref, outgoing.at[0], stage_sem.at[0]),
         pltpu.make_async_copy(grads_ref, outgoing.at[1], stage_sem.at[1]),
@@ -299,49 +310,51 @@
         copy.start()
     for copy in loads:
         copy.start()
-    barrier = pltpu.get_barrier_semaphore()
-
-    def greet(peer):
-        pl.semaphore_signal(barrier, inc=1, device_id={"seq": peer}, device_id_type=MESH)
-
-    per_peer(me, greet)
-    for step in range(1, 4):
-        pl.semaphore_signal(
-            barrier, inc=1, device_id={"ch": (row + step) % 4}, device_id_type=MESH
-        )
     for copy in stages:
         copy.wait()
     pl.semaphore_wait(barrier, OWNERS - 1 + 3)
 
-    def exchange(source, target, send, receive):
-        def action(peer):
-            pltpu.make_async_remote_copy(
-                src_ref=source(peer),
-                dst_ref=target,
-                send_sem=send,
-                recv_sem=receive,
-                device_id={"seq": peer},
-                device_id_type=MESH,
-            ).start()
-
-        per_peer(me, action)
+    def send(source, target, sent, received, device):
+        pltpu.make_async_remote_copy(
+            src_ref=source,
+            dst_ref=target,
+            send_sem=sent,
+            recv_sem=received,
+            device_id=device,
+            device_id_type=MESH,
+        ).start()
 
     own = pltpu.make_async_copy(outgoing.at[:, me], arrived.at[:, me], own_sem.at[0])
     own.start()
-    exchange(lambda peer: outgoing.at[:, peer], arrived.at[:, me], send_sem.at[0], signal_sem)
+    per_peer(
+        me,
+        lambda peer: send(
+            outgoing.at[:, peer], arrived.at[:, me], send_sem.at[0], signal_sem, {"seq": peer}
+        ),
+    )
 
     lane_row = lax.broadcasted_iota(jnp.int32, (1, WIDTH), 1)
-    step_row = jnp.exp(
-        jnp.where(lane_row < STATES, log_step_ref[2 * me], log_step_ref[2 * me + 1])
-    )
-    decay_row = states_ref[0:1, :]
-    turn_row = states_ref[1:2, :]
-    readout = (readout_ref[0, pl.ds(me, 1), :], readout_ref[1, pl.ds(me, 1), :])
+    left = lane_row < STATES
+    step_row = jnp.exp(jnp.where(left, log_step_ref[2 * me], log_step_ref[2 * me + 1]))
+    decay_row = jnp.concatenate([decay_ref[...], decay_ref[...]], axis=1)
+    turn_row = jnp.concatenate([rotation_ref[...], rotation_ref[...]], axis=1)
+    readout_turned[...] = jnp.transpose(
+        jnp.concatenate([readout_ref[0], readout_ref[1]], axis=0), (1, 0)
+    )
+    low = readout_turned[pl.ds(2 * me, 1), :]
+    high = readout_turned[pl.ds(2 * me + 1, 1), :]
+    readout = (
+        jnp.where(left, low, pltpu.roll(high, STATES, 1)),
+        jnp.where(left, pltpu.roll(low, STATES, 1), high),
+    )
     primal = primal_rows(step_row, decay_row, turn_row, readout)
     offsets = lax.broadcasted_iota(jnp.int32, (WIDTH, WIDTH), 0).astype(jnp.float32)
     starts = offsets * float(WIDTH)
     near = power_table(primal["rate"], offsets)
     base = power_table(primal["rate"], starts)
+    tables = halves(
+        jnp.concatenate([near[0], near[1], offsets * near[0], offsets * near[1]], axis=1)
+    )
     for copy in loads:
         copy.wait()
 
@@ -355,116 +368,179 @@
     lags = correlate(signals, first, turns, second, third, fourth)
     lag_rows[:, 0, :] = lags[:, :WIDTH]
     lag_rows[:, 1, :] = lags[:, WIDTH:]
-    own_lags = pltpu.make_async_copy(lag_rows.at[me], lags_out.at[me], own_sem.at[1])
+
+    powers, lag_powers = power_sums(lags, tables, base, starts, norm_scale)
+    readout_grad, step_terms, state_grad = parameter_rows(primal, readout, powers, lag_powers)
+    cross_rows[...] = jnp.where(
+        left,
+        state_grad[0] + pltpu.roll(state_grad[0], STATES, 1),
+        state_grad[1] + pltpu.roll(state_grad[1], STATES, 1),
+    )
+    readout_rows[0] = readout_grad[0]
+    readout_rows[1] = readout_grad[1]
+    cross_in[row] = cross_rows[...]
+    for other in rows_across:
+        send(cross_rows, cross_in.at[row], send_sem.at[3], cross_sem, {"ch": other})
+    own_readout = pltpu.make_async_copy(readout_rows, readout_out.at[:, me], own_sem.at[1])
+    own_readout.start()
+    own_lags = pltpu.make_async_copy(lag_rows.at[me], lags_out.at[me], own_sem.at[2])
     own_lags.start()
-    exchange(lambda peer: lag_rows.at[peer], lags_out.at[me], send_sem.at[1], lag_sem)
-
-    powers, lag_powers = power_sums(lags, near, base, starts, offsets, norm_scale)
-    readout_grad, step_terms, state_grad = parameter_rows(primal, readout, powers, lag_powers)
-    step_grad = jnp.where(
-        lane_row < STATES,
-        jnp.sum(jnp.where(lane_row < STATES, step_terms, 0.0), axis=1, keepdims=True),
-        jnp.sum(jnp.where(lane_row < STATES, 0.0, step_terms), axis=1, keepdims=True),
-    )
-    param_rows[0:1, :] = readout_grad[0]
-    param_rows[1:2, :] = readout_grad[1]
-    param_rows[2:3, :] = step_grad
-    param_rows[3:4, :] = jnp.zeros_like(step_grad)
-    own_params = pltpu.make_async_copy(param_rows, params_out.at[me], own_sem.at[2])
-    own_params.start()
-    state_rows[0:1, :] = state_grad[0]
-    state_rows[1:2, :] = state_grad[1]
-    crossings = [
-        pltpu.make_async_remote_copy(
-            src_ref=state_rows,
-            dst_ref=state_in.at[step - 1],
-            send_sem=cross_send_sem.at[step - 1],
-            recv_sem=cross_sem.at[step - 1],
-            device_id={"ch": (row + step) % 4},
-            device_id_type=MESH,
+    per_peer(
+        me,
+        lambda peer: send(
+            lag_rows.at[peer], lags_out.at[me], send_sem.at[1], lag_sem, {"seq": peer}
+        ),
+    )
+
+    first_step = jnp.sum(jnp.where(left, step_terms, 0.0), axis=1, keepdims=True)
+    second_step = jnp.sum(jnp.where(left, 0.0, step_terms), axis=1, keepdims=True)
+    count = WIDTH * lax.broadcasted_iota(jnp.int32, (2, WIDTH), 0) + lax.broadcasted_iota(
+        jnp.int32, (2, WIDTH), 1
+    )
+    line_rows[0:2, :] = jnp.where(
+        count == 2 * me, first_step, jnp.where(count == 2 * me + 1, second_step, 0.0)
+    )
+    part = cross_in.at[pl.ds(0, 3)]
+    pltpu.make_async_copy(part, part, cross_sem).wait()
+    line_rows[2:3, :] = (cross_in[0] + cross_in[1]) + (cross_in[2] + cross_in[3])
+    line_rows[3:4, :] = jnp.zeros_like(step_row)
+    line_in[2 * y + core] = line_rows[...]
+    line = [
+        16 * at_y + 2 * z + at_core
+        for at_y in ring_places(y, 8)
+        for at_core in (1 - core, core)
+    ]
+    for peer in line[:-1]:
+        send(line_rows, line_in.at[2 * y + core], send_sem.at[4], line_sem, {"seq": peer})
+    per_peer(
+        me,
+        lambda peer: send(
+            readout_rows, readout_out.at[:, me], send_sem.at[2], readout_sem, {"seq": peer}
+        ),
+    )
+    part = line_in.at[pl.ds(0, 15)]
+    pltpu.make_async_copy(part, part, line_sem).wait()
+    column_rows[...] = sum_in_order(line_in, 16)
+    column_in[z] = column_rows[...]
+    for at_z in ring_places(z, 8)[:7]:
+        send(
+            column_rows,
+            column_in.at[z],
+            send_sem.at[5],
+            column_sem,
+            {"seq": 16 * y + 2 * at_z + core},
         )
-        for step in range(1, 4)
-    ]
-    for copy in crossings:
-        copy.start()
-    exchange(lambda peer: param_rows, params_out.at[me], send_sem.at[2], param_sem)
-    for copy in crossings:
-        copy.wait()
-    state_sums[...] = state_rows[...] + state_in[1] + (state_in[0] + state_in[2])
-    own_state = pltpu.make_async_copy(state_sums, shared_out.at[me], own_sem.at[3])
-    own_state.start()
-    exchange(lambda peer: state_sums, shared_out.at[me], send_sem.at[3], state_sem)
-
-    for copy in (own_lags, own_params, own_state):
-        copy.wait()
-    for buffer, semaphore in (
-        (lags_out, lag_sem),
-        (params_out, param_sem),
-        (shared_out, state_sem),
-    ):
-        part = buffer.at[pl.ds(0, OWNERS - 1)]
-        pltpu.make_async_copy(part, part, semaphore).wait()
+    part = column_in.at[pl.ds(0, 7)]
+    pltpu.make_async_copy(part, part, column_sem).wait()
+    sums_out[...] = sum_in_order(column_in, 8)
+
+    own_lags.wait()
+    own_readout.wait()
+    part = lags_out.at[pl.ds(0, OWNERS - 1)]
+    pltpu.make_async_copy(part, part, lag_sem).wait()
+    pltpu.make_async_copy(part, part, send_sem.at[1]).wait()
+    part = readout_out.at[:, pl.ds(0, OWNERS - 1)]
+    pltpu.make_async_copy(part, part, readout_sem).wait()
+    pltpu.make_async_copy(part, part, send_sem.at[2]).wait()
     pltpu.make_async_copy(rest, rest, send_sem.at[0]).wait()
-    for buffer, place in ((lags_out, 1), (params_out, 2), (shared_out, 3)):
-        part = buffer.at[pl.ds(0, OWNERS - 1)]
+    for buffer, count_sent, place in ((cross_in, 3, 3), (line_in, 15, 4), (column_in, 7, 5)):
+        part = buffer.at[pl.ds(0, count_sent)]
         pltpu.make_async_copy(part, part, send_sem.at[place]).wait()
+
+
+def sum_in_order(buffer, count):
+    parts = [buffer[place] for place in range(count)]
+    while len(parts) > 1:
+        parts = [parts[place] + parts[place + 1] for place in range(0, len(parts), 2)]
+    return parts[0]
+
+
+def finish(lags_ref, readout_ref, sums_ref, lags_out, readout_out, step_out, state_out):
+    lags_out[...] = lags_ref[...]
+    blocks = []
+    for part in range(2):
+        turned = jnp.transpose(readout_ref[part], (1, 0))
+        blocks.append(jnp.concatenate([turned[:STATES], turned[STATES:]], axis=1))
+    value = jnp.concatenate(blocks, axis=0)
+    at_row = lax.broadcasted_iota(jnp.int32, (2 * OWNERS, 2 * OWNERS), 0)
+    at_column = lax.broadcasted_iota(jnp.int32, (2 * OWNERS, 2 * OWNERS), 1)
+    places = 2 * (at_row % OWNERS) + at_row // OWNERS
+    order = jnp.where(at_column == places, 1.0, 0.0).astype(jnp.bfloat16)
+    high = value.astype(jnp.bfloat16)
+    left = value - high.astype(jnp.float32)
+    middle, low = halves(left)
+    sorted_ = dot(high, order) + (dot(middle, order) + dot(low, order))
+    readout_out[0] = sorted_[:STATES]
+    readout_out[1] = sorted_[STATES:]
+    step_out[...] = sums_ref[0:2, :]
+    state_out[0:1, :] = sums_ref[2:3, :STATES]
+    state_out[1:2, :] = sums_ref[2:3, STATES:]
 
 
 def per_device(tables, inputs, out_grad, readout, log_step, decay_log, rotation):
     norm_scale = 1.0 / math.sqrt(LENGTH)
-    states = jnp.stack(
-        [jnp.concatenate([decay_log, decay_log]), jnp.concatenate([rotation, rotation])]
-    )
     dma = pltpu.SemaphoreType.DMA
     any_space = pl.BlockSpec(memory_space=pl.ANY)
     vmem = pl.BlockSpec(memory_space=pltpu.VMEM)
     smem = pl.BlockSpec(memory_space=pltpu.SMEM)
-    lags, params, shared = pl.pallas_call(
+    f32 = jnp.float32
+    lags, readout_rows, sums = pl.pallas_call(
         functools.partial(kernel, norm_scale),
         out_shape=(
-            jax.ShapeDtypeStruct((OWNERS, 2, WIDTH), jnp.float32),
-            jax.ShapeDtypeStruct((OWNERS, 4, WIDTH), jnp.float32),
-            jax.ShapeDtypeStruct((OWNERS, 2, WIDTH), jnp.float32),
+            jax.ShapeDtypeStruct((OWNERS, 2, WIDTH), f32),
+            jax.ShapeDtypeStruct((2, OWNERS, 1, WIDTH), f32),
+            jax.ShapeDtypeStruct((4, WIDTH), f32),
         ),
-        in_specs=[any_space, any_space, vmem, smem, vmem] + [any_space] * 5,
+        in_specs=[any_space, any_space, vmem, smem, vmem, vmem] + [any_space] * 5,
         out_specs=(vmem, vmem, vmem),
         scratch_shapes=[
             pltpu.VMEM((2, OWNERS, 2, WIDTH), jnp.bfloat16),
             pltpu.VMEM((2, OWNERS, 2, WIDTH), jnp.bfloat16),
-            pltpu.VMEM((OWNERS, 2, WIDTH), jnp.float32),
-            pltpu.VMEM((4, WIDTH), jnp.float32),
-            pltpu.VMEM((2, WIDTH), jnp.float32),
-            pltpu.VMEM((2, WIDTH), jnp.float32),
-            pltpu.VMEM((3, 2, WIDTH), jnp.float32),
+            pltpu.VMEM((OWNERS, 2, WIDTH), f32),
+            pltpu.VMEM((2, 1, WIDTH), f32),
+            pltpu.VMEM((2 * OWNERS, WIDTH), f32),
+            pltpu.VMEM((1, WIDTH), f32),
+            pltpu.VMEM((4, 1, WIDTH), f32),
+            pltpu.VMEM((4, WIDTH), f32),
+            pltpu.VMEM((16, 4, WIDTH), f32),
+            pltpu.VMEM((4, WIDTH), f32),
+            pltpu.VMEM((8, 4, WIDTH), f32),
         ]
         + [pltpu.VMEM(table.shape, table.dtype) for table in tables]
-        + [
-            dma((2,)),
-            dma((5,)),
-            dma((4,)),
-            dma((4,)),
-            dma,
-            dma,
-            dma,
-            dma,
-            dma((3,)),
-            dma((3,)),
-        ],
+        + [dma((2,)), dma((5,)), dma((3,)), dma((6,)), dma, dma, dma, dma, dma, dma],
         compiler_params=pltpu.CompilerParams(collective_id=0, has_side_effects=True),
         name="channel_rows",
     )(
         inputs.reshape(OWNERS, 2, WIDTH),
         out_grad.reshape(OWNERS, 2, WIDTH),
-        readout.reshape(2, OWNERS, WIDTH),
+        jnp.transpose(readout, (0, 2, 1)),
         log_step,
-        states,
+        decay_log.reshape(1, STATES),
+        rotation.reshape(1, STATES),
         *[jnp.asarray(table) for table in tables],
     )
-    kernel_grad = lags.reshape(2 * OWNERS, WIDTH)
-    readout_grad = jnp.transpose(params[:, :2, :], (1, 0, 2)).reshape(2, 2 * OWNERS, STATES)
-    step_grad = params[:, 2, :].reshape(2 * OWNERS, STATES)[:, 0]
-    state = jnp.sum(shared, axis=0).reshape(2, 2, STATES)
-    return kernel_grad, readout_grad, step_grad, state[:, 0] + state[:, 1]
+    kernel_grad, readout_grad, step_grad, state_grad = pl.pallas_call(
+        finish,
+        out_shape=(
+            jax.ShapeDtypeStruct((2 * OWNERS, WIDTH), f32),
+            jax.ShapeDtypeStruct((2, STATES, 2 * OWNERS), f32),
+            jax.ShapeDtypeStruct((2, WIDTH), f32),
+            jax.ShapeDtypeStruct((2, STATES), f32),
+        ),
+        in_specs=[vmem] * 3,
+        out_specs=(vmem,) * 4,
+        name="finish",
+    )(
+        lags.reshape(2 * OWNERS, WIDTH),
+        readout_rows.reshape(2, OWNERS, WIDTH),
+        sums,
+    )
+    return (
+        kernel_grad,
+        jnp.transpose(readout_grad, (0, 2, 1)),
+        step_grad.reshape(2 * OWNERS),
+        state_grad,
+    )
 
 
 def solution(mesh):

time: 65.5 us -> 43.3 us (0.66)
  Pallas kernels: 56.1 us -> 42.5 us
  local copies, waits for them, and re-layouts: 6.13 us -> 0 us
  other arithmetic: 2.31 us -> 0 us
    pallas_call x1, Pallas kernels: 56.1 us -> 40.6 us  [per_device(): pl.pallas_call(functools.partial(kernel, norm_scale), out_shape=(jax.Shap...]
    unnamed x11 -> x0, local copies, waits for them, and re-layouts: 3.24 us -> none
    pallas_call x0 -> x1, Pallas kernels: none -> 1.91 us  [per_device(): pl.pallas_call(finish, out_shape=(jax.ShapeDtypeStruct((2 * OWNERS, WIDTH...]
    slice x2 -> x0, local copies, waits for them, and re-layouts: 1.82 us -> none  [per_device(): step_grad = params[:, 2, :].reshape(2 * OWNERS, STATES)[:, 0]]
    reduce_sum x1 -> x0, other arithmetic: 1.09 us -> none  [per_device(): state = jnp.sum(shared, axis=0).reshape(2, 2, STATES)]
    reshape x3 -> x0, local copies, waits for them, and re-layouts: 0.94 us -> none  [the longest x1 0.76 us: per_device(): readout.reshape(2, OWNERS, WIDTH)]
where the time goes in v2:
time: 43.3 us; the launch traced here: 43.1 us
  Pallas kernels  42.5 us (98%)
  between operations  0.64 us (1%)
    pallas_call x1, Pallas kernels, per_device(): pl.pallas_call(functools.partial(kernel, norm_scale), out_shape=(jax.Shap...  40.6 us
    pallas_call x1, Pallas kernels, per_device(): pl.pallas_call(finish, out_shape=(jax.ShapeDtypeStruct((2 * OWNERS, WIDTH...  1.91 us

profile of v2, /device:TPU:1, one launch (start us, length us, event | category | flops | bytes accessed | tf_op | source)
XLA Modules:
  0.0 43.1 jit_solution(11440186253345180490)
XLA Ops:
  0.6 40.6 %channel_rows.1 = (f32[128,2,128]{2,1,0:T(2,128)}, f32[2,128,1,128]{3,2,1,0:T(1,128)}, f32[4,128]{1,0:T(4,128)}) custom-call(bf16[128,2,128]{2,1,0:T(2,128)(2,1)} %bitcast.12, bf16[128,2,128]{2,1,0:T(2,128)(2,1)} %bitcast.13, f32[2,64,256]{2,1,0:T(8,128)} %bitcast.9, f32[256]{0:T(256)} %log_step_ref.1, f32[1,64]{1,0:T(1,128)} %bitcast.14, f32[1,64]{1,0:T(1,128)} %bitcast.15, ...), custom_call_target="tpu_custom_call" | custom-call | tf_op jit(solution)/shard_map/channel_rows/pallas_call | solution.py:487
  41.2 1.9 %finish.1 = (f32[256,128]{1,0:T(8,128)}, f32[2,64,256]{2,1,0:T(8,128)}, f32[2,128]{1,0:T(2,128)}, f32[2,64]{1,0:T(2,128)}) custom-call(f32[256,128]{1,0:T(8,128)} %bitcast.10, f32[2,128,128]{2,1,0:T(8,128)} %bitcast.11, f32[4,128]{1,0:T(4,128)} %get-tuple-element.13.sums_ref), custom_call_target="tpu_custom_call" | custom-call | tf_op jit(solution)/shard_map/finish/pallas_call | solution.py:522

commit v3 on v2

--- a/solution.py
+++ b/solution.py
@@ -239,10 +239,10 @@
     norm_scale,
     inputs_ref,
     grads_ref,
-    readout_ref,
-    log_step_ref,
-    decay_ref,
-    rotation_ref,
+    readout_in,
+    log_step_in,
+    decay_in,
+    rotation_in,
     first_ref,
     turns_ref,
     second_ref,
@@ -262,6 +262,10 @@
     line_in,
     column_rows,
     column_in,
+    readout_ref,
+    log_step_ref,
+    decay_ref,
+    rotation_ref,
     first,
     turns,
     second,
@@ -281,6 +285,12 @@
     me = lax.axis_index("seq")
     row = lax.axis_index("ch")
     y, z, core = place_of(me)
+    stages = [
+        pltpu.make_async_copy(inputs_ref, outgoing.at[0], stage_sem.at[0]),
+        pltpu.make_async_copy(grads_ref, outgoing.at[1], stage_sem.at[1]),
+    ]
+    for copy in stages:
+        copy.start()
     barrier = pltpu.get_barrier_semaphore()
 
     def greet(peer):
@@ -290,14 +300,14 @@
     rows_across = [(row + step) % 4 for step in range(1, 4)]
     for other in rows_across:
         pl.semaphore_signal(barrier, inc=1, device_id={"ch": other}, device_id_type=MESH)
-    stages = [
-        pltpu.make_async_copy(inputs_ref, outgoing.at[0], stage_sem.at[0]),
-        pltpu.make_async_copy(grads_ref, outgoing.at[1], stage_sem.at[1]),
-    ]
     loads = [
         pltpu.make_async_copy(source, target, table_sem.at[place])
         for place, (source, target) in enumerate(
             (
+                (log_step_in, log_step_ref),
+                (decay_in, decay_ref),
+                (rotation_in, rotation_ref),
+                (readout_in, readout_ref),
                 (first_ref, first),
                 (turns_ref, turns),
                 (second_ref, second),
@@ -306,8 +316,6 @@
             )
         )
     ]
-    for copy in stages:
-        copy.start()
     for copy in loads:
         copy.start()
     for copy in stages:
@@ -333,6 +341,8 @@
         ),
     )
 
+    for copy in loads[:4]:
+        copy.wait()
     lane_row = lax.broadcasted_iota(jnp.int32, (1, WIDTH), 1)
     left = lane_row < STATES
     step_row = jnp.exp(jnp.where(left, log_step_ref[2 * me], log_step_ref[2 * me + 1]))
@@ -355,7 +365,7 @@
     tables = halves(
         jnp.concatenate([near[0], near[1], offsets * near[0], offsets * near[1]], axis=1)
     )
-    for copy in loads:
+    for copy in loads[4:]:
         copy.wait()
 
     own.wait()
@@ -381,9 +391,27 @@
     cross_in[row] = cross_rows[...]
     for other in rows_across:
         send(cross_rows, cross_in.at[row], send_sem.at[3], cross_sem, {"ch": other})
-    own_readout = pltpu.make_async_copy(readout_rows, readout_out.at[:, me], own_sem.at[1])
-    own_readout.start()
-    own_lags = pltpu.make_async_copy(lag_rows.at[me], lags_out.at[me], own_sem.at[2])
+    readout_out[0, y, z, core] = readout_grad[0]
+    readout_out[1, y, z, core] = readout_grad[1]
+    around_y = ring_places(y, 8)
+    around_z = ring_places(z, 8)
+    for at_y in around_y[:-1]:
+        send(
+            readout_rows.at[0],
+            readout_out.at[0, y, z, core],
+            send_sem.at[2],
+            readout_sem.at[0],
+            {"seq": 16 * at_y + 2 * z + core},
+        )
+    for at_z in around_z[:-1]:
+        send(
+            readout_rows.at[1],
+            readout_out.at[1, y, z, core],
+            send_sem.at[6],
+            readout_sem.at[1],
+            {"seq": 16 * y + 2 * at_z + core},
+        )
+    own_lags = pltpu.make_async_copy(lag_rows.at[me], lags_out.at[me], own_sem.at[1])
     own_lags.start()
     per_peer(
         me,
@@ -405,24 +433,24 @@
     line_rows[2:3, :] = (cross_in[0] + cross_in[1]) + (cross_in[2] + cross_in[3])
     line_rows[3:4, :] = jnp.zeros_like(step_row)
     line_in[2 * y + core] = line_rows[...]
-    line = [
-        16 * at_y + 2 * z + at_core
-        for at_y in ring_places(y, 8)
-        for at_core in (1 - core, core)
-    ]
+    line = [16 * at_y + 2 * z + at_core for at_y in around_y for at_core in (1 - core, core)]
+    column = [16 * y + 2 * at_z + at_core for at_z in around_z for at_core in (1 - core, core)]
     for peer in line[:-1]:
         send(line_rows, line_in.at[2 * y + core], send_sem.at[4], line_sem, {"seq": peer})
-    per_peer(
-        me,
-        lambda peer: send(
-            readout_rows, readout_out.at[:, me], send_sem.at[2], readout_sem, {"seq": peer}
-        ),
-    )
+    real_line = readout_out.at[0, :, z, core]
+    imag_line = readout_out.at[1, y, :, core]
+    real_seven = readout_out.at[0, pl.ds(0, 7), 0, 0]
+    pltpu.make_async_copy(real_seven, real_seven, readout_sem.at[0]).wait()
+    for peer in column[:-1]:
+        send(real_line, real_line, send_sem.at[7], readout_sem.at[2], {"seq": peer})
+    pltpu.make_async_copy(real_seven, real_seven, readout_sem.at[1]).wait()
+    for peer in line[:-1]:
+        send(imag_line, imag_line, send_sem.at[8], readout_sem.at[3], {"seq": peer})
     part = line_in.at[pl.ds(0, 15)]
     pltpu.make_async_copy(part, part, line_sem).wait()
     column_rows[...] = sum_in_order(line_in, 16)
     column_in[z] = column_rows[...]
-    for at_z in ring_places(z, 8)[:7]:
+    for at_z in around_z[:-1]:
         send(
             column_rows,
             column_in.at[z],
@@ -435,13 +463,16 @@
     sums_out[...] = sum_in_order(column_in, 8)
 
     own_lags.wait()
-    own_readout.wait()
     part = lags_out.at[pl.ds(0, OWNERS - 1)]
     pltpu.make_async_copy(part, part, lag_sem).wait()
     pltpu.make_async_copy(part, part, send_sem.at[1]).wait()
-    part = readout_out.at[:, pl.ds(0, OWNERS - 1)]
-    pltpu.make_async_copy(part, part, readout_sem).wait()
-    pltpu.make_async_copy(part, part, send_sem.at[2]).wait()
+    part = readout_out.at[0].reshape(16, 8, 1, WIDTH).at[pl.ds(0, 15)]
+    pltpu.make_async_copy(part, part, readout_sem.at[2]).wait()
+    pltpu.make_async_copy(part, part, readout_sem.at[3]).wait()
+    pltpu.make_async_copy(part, part, send_sem.at[7]).wait()
+    pltpu.make_async_copy(part, part, send_sem.at[8]).wait()
+    pltpu.make_async_copy(real_seven, real_seven, send_sem.at[2]).wait()
+    pltpu.make_async_copy(real_seven, real_seven, send_sem.at[6]).wait()
     pltpu.make_async_copy(rest, rest, send_sem.at[0]).wait()
     for buffer, count_sent, place in ((cross_in, 3, 3), (line_in, 15, 4), (column_in, 7, 5)):
         part = buffer.at[pl.ds(0, count_sent)]
@@ -455,8 +486,11 @@
     return parts[0]
 
 
-def finish(lags_ref, readout_ref, sums_ref, lags_out, readout_out, step_out, state_out):
-    lags_out[...] = lags_ref[...]
+def finish(
+    lags_ref, readout_ref, sums_ref, lags_out, readout_out, step_out, state_out, lag_sem
+):
+    lags = pltpu.make_async_copy(lags_ref, lags_out, lag_sem)
+    lags.start()
     blocks = []
     for part in range(2):
         turned = jnp.transpose(readout_ref[part], (1, 0))
@@ -475,6 +509,11 @@
     step_out[...] = sums_ref[0:2, :]
     state_out[0:1, :] = sums_ref[2:3, :STATES]
     state_out[1:2, :] = sums_ref[2:3, STATES:]
+    lags.wait()
+
+
+def keep(value):
+    return pltpu.with_memory_space_constraint(value, pltpu.VMEM)
 
 
 def per_device(tables, inputs, out_grad, readout, log_step, decay_log, rotation):
@@ -482,16 +521,15 @@
     dma = pltpu.SemaphoreType.DMA
     any_space = pl.BlockSpec(memory_space=pl.ANY)
     vmem = pl.BlockSpec(memory_space=pltpu.VMEM)
-    smem = pl.BlockSpec(memory_space=pltpu.SMEM)
     f32 = jnp.float32
     lags, readout_rows, sums = pl.pallas_call(
         functools.partial(kernel, norm_scale),
         out_shape=(
-            jax.ShapeDtypeStruct((OWNERS, 2, WIDTH), f32),
-            jax.ShapeDtypeStruct((2, OWNERS, 1, WIDTH), f32),
-            jax.ShapeDtypeStruct((4, WIDTH), f32),
+            pltpu.VMEM((OWNERS, 2, WIDTH), f32),
+            pltpu.VMEM((2, 8, 8, 2, 1, WIDTH), f32),
+            pltpu.VMEM((4, WIDTH), f32),
         ),
-        in_specs=[any_space, any_space, vmem, smem, vmem, vmem] + [any_space] * 5,
+        in_specs=[any_space] * 11,
         out_specs=(vmem, vmem, vmem),
         scratch_shapes=[
             pltpu.VMEM((2, OWNERS, 2, WIDTH), jnp.bfloat16),
@@ -506,8 +544,14 @@
             pltpu.VMEM((4, WIDTH), f32),
             pltpu.VMEM((8, 4, WIDTH), f32),
         ]
+        + [
+            pltpu.VMEM((2, STATES, 2 * OWNERS), f32),
+            pltpu.SMEM((2 * OWNERS,), f32),
+            pltpu.VMEM((1, STATES), f32),
+            pltpu.VMEM((1, STATES), f32),
+        ]
         + [pltpu.VMEM(table.shape, table.dtype) for table in tables]
-        + [dma((2,)), dma((5,)), dma((3,)), dma((6,)), dma, dma, dma, dma, dma, dma],
+        + [dma((2,)), dma((9,)), dma((2,)), dma((9,)), dma, dma, dma((4,)), dma, dma, dma],
         compiler_params=pltpu.CompilerParams(collective_id=0, has_side_effects=True),
         name="channel_rows",
     )(
@@ -528,12 +572,13 @@
             jax.ShapeDtypeStruct((2, STATES), f32),
         ),
         in_specs=[vmem] * 3,
-        out_specs=(vmem,) * 4,
+        out_specs=(any_space, vmem, vmem, vmem),
+        scratch_shapes=[dma],
         name="finish",
     )(
-        lags.reshape(2 * OWNERS, WIDTH),
-        readout_rows.reshape(2, OWNERS, WIDTH),
-        sums,
+        keep(lags.reshape(2 * OWNERS, WIDTH)),
+        keep(readout_rows.reshape(2, OWNERS, WIDTH)),
+        keep(sums),
     )
     return (
         kernel_grad,

time: 43.3 us -> 41.1 us (0.949)
  Pallas kernels: 42.5 us -> 40.3 us
    pallas_call x1, Pallas kernels: 40.6 us -> 39 us  [per_device(): pl.pallas_call(functools.partial(kernel, norm_scale), out_shape=(pltpu.VM...]
    pallas_call x1, Pallas kernels: 1.91 us -> 1.33 us  [per_device(): pl.pallas_call(finish, out_shape=(jax.ShapeDtypeStruct((2 * OWNERS, WIDTH...]
where the time goes in v3:
time: 41.1 us; the launch traced here: 40.9 us
  Pallas kernels  40.3 us (98%)
  between operations  0.64 us (2%)
    pallas_call x1, Pallas kernels, per_device(): pl.pallas_call(functools.partial(kernel, norm_scale), out_shape=(pltpu.VM...  39 us
    pallas_call x1, Pallas kernels, per_device(): pl.pallas_call(finish, out_shape=(jax.ShapeDtypeStruct((2 * OWNERS, WIDTH...  1.33 us

profile of v3, /device:TPU:1, one launch (start us, length us, event | category | flops | bytes accessed | tf_op | source)
XLA Modules:
  0.0 40.9 jit_solution(7912443255787985989)
XLA Ops:
  0.6 39.0 %channel_rows.1 = (f32[128,2,128]{2,1,0:T(2,128)S(1)}, f32[2,8,8,2,1,128]{5,4,3,2,1,0:T(1,128)S(1)}, f32[4,128]{1,0:T(4,128)S(1)}) custom-call(bf16[128,2,128]{2,1,0:T(2,128)(2,1)} %bitcast.12, bf16[128,2,128]{2,1,0:T(2,128)(2,1)} %bitcast.13, f32[2,64,256]{2,1,0:T(8,128)} %bitcast.11, f32[256]{0:T(256)} %log_step_in.1, f32[1,64]{1,0:T(1,128)} %bitcast.14, ...), custom_call_target="tpu_custom_call" | custom-call | tf_op jit(solution)/shard_map/channel_rows/pallas_call | solution.py:525
  39.6 1.3 %finish.1 = (f32[256,128]{1,0:T(8,128)}, f32[2,64,256]{2,1,0:T(8,128)}, f32[2,128]{1,0:T(2,128)}, f32[2,64]{1,0:T(2,128)}) custom-call(f32[256,128]{1,0:T(8,128)S(1)} %bitcast.9, f32[2,128,128]{2,1,0:T(8,128)S(1)} %bitcast.10, f32[4,128]{1,0:T(4,128)S(1)} %get-tuple-element.13.sums_ref), custom_call_target="tpu_custom_call" | custom-call | tf_op jit(solution)/shard_map/finish/pallas_call | solution.py:566

commit v4 on v3

--- a/solution.py
+++ b/solution.py
@@ -249,17 +249,19 @@
     third_ref,
     fourth_ref,
     lags_out,
-    readout_out,
-    sums_out,
+    sorted_out,
+    step_out,
+    state_out,
     outgoing,
     arrived,
     lag_rows,
     readout_rows,
+    readout_all,
     readout_turned,
-    cross_rows,
-    cross_in,
-    line_rows,
-    line_in,
+    state_rows,
+    state_in,
+    step_rows,
+    step_in,
     column_rows,
     column_in,
     readout_ref,
@@ -278,8 +280,8 @@
     signal_sem,
     lag_sem,
     readout_sem,
-    cross_sem,
-    line_sem,
+    state_sem,
+    step_sem,
     column_sem,
 ):
     me = lax.axis_index("seq")
@@ -297,9 +299,14 @@
         pl.semaphore_signal(barrier, inc=1, device_id={"seq": peer}, device_id_type=MESH)
 
     per_peer(me, greet)
-    rows_across = [(row + step) % 4 for step in range(1, 4)]
-    for other in rows_across:
-        pl.semaphore_signal(barrier, inc=1, device_id={"ch": other}, device_id_type=MESH)
+    around_y = ring_places(y, 8)
+    around_z = ring_places(z, 8)
+    around_x = [(row + step) % 4 for step in (2, 1, 3, 0)]
+    across = [(at_x, 16 * at_y + 2 * z + core) for at_x in around_x[:3] for at_y in around_y]
+    for at_x, peer in across:
+        pl.semaphore_signal(
+            barrier, inc=1, device_id={"ch": at_x, "seq": peer}, device_id_type=MESH
+        )
     loads = [
         pltpu.make_async_copy(source, target, table_sem.at[place])
         for place, (source, target) in enumerate(
@@ -320,7 +327,7 @@
         copy.start()
     for copy in stages:
         copy.wait()
-    pl.semaphore_wait(barrier, OWNERS - 1 + 3)
+    pl.semaphore_wait(barrier, OWNERS - 1 + len(across))
 
     def send(source, target, sent, received, device):
         pltpu.make_async_remote_copy(
@@ -381,36 +388,52 @@
 
     powers, lag_powers = power_sums(lags, tables, base, starts, norm_scale)
     readout_grad, step_terms, state_grad = parameter_rows(primal, readout, powers, lag_powers)
-    cross_rows[...] = jnp.where(
+    state_rows[...] = jnp.where(
         left,
         state_grad[0] + pltpu.roll(state_grad[0], STATES, 1),
         state_grad[1] + pltpu.roll(state_grad[1], STATES, 1),
     )
+    line = [16 * at_y + 2 * z + core for at_y in around_y[:-1]]
+    for at_x, peer in across + [(around_x[3], peer) for peer in line]:
+        send(
+            state_rows,
+            state_in.at[row, y],
+            send_sem.at[3],
+            state_sem,
+            {"ch": at_x, "seq": peer},
+        )
+    state_in[row, y] = state_rows[...]
+    first_step = jnp.sum(jnp.where(left, step_terms, 0.0), axis=1, keepdims=True)
+    second_step = jnp.sum(jnp.where(left, 0.0, step_terms), axis=1, keepdims=True)
+    count = WIDTH * lax.broadcasted_iota(jnp.int32, (2, WIDTH), 0) + lax.broadcasted_iota(
+        jnp.int32, (2, WIDTH), 1
+    )
+    step_rows[...] = jnp.where(
+        count == 2 * me, first_step, jnp.where(count == 2 * me + 1, second_step, 0.0)
+    )
+    step_in[y] = step_rows[...]
     readout_rows[0] = readout_grad[0]
     readout_rows[1] = readout_grad[1]
-    cross_in[row] = cross_rows[...]
-    for other in rows_across:
-        send(cross_rows, cross_in.at[row], send_sem.at[3], cross_sem, {"ch": other})
-    readout_out[0, y, z, core] = readout_grad[0]
-    readout_out[1, y, z, core] = readout_grad[1]
-    around_y = ring_places(y, 8)
-    around_z = ring_places(z, 8)
-    for at_y in around_y[:-1]:
+    readout_all[0, y, z, core] = readout_grad[0]
+    readout_all[1, y, z, core] = readout_grad[1]
+    for peer in line:
         send(
             readout_rows.at[0],
-            readout_out.at[0, y, z, core],
+            readout_all.at[0, y, z, core],
             send_sem.at[2],
             readout_sem.at[0],
-            {"seq": 16 * at_y + 2 * z + core},
+            {"seq": peer},
         )
     for at_z in around_z[:-1]:
         send(
             readout_rows.at[1],
-            readout_out.at[1, y, z, core],
+            readout_all.at[1, y, z, core],
             send_sem.at[6],
             readout_sem.at[1],
             {"seq": 16 * y + 2 * at_z + core},
         )
+    for peer in line:
+        send(step_rows, step_in.at[y], send_sem.at[4], step_sem, {"seq": peer})
     own_lags = pltpu.make_async_copy(lag_rows.at[me], lags_out.at[me], own_sem.at[1])
     own_lags.start()
     per_peer(
@@ -420,63 +443,52 @@
         ),
     )
 
-    first_step = jnp.sum(jnp.where(left, step_terms, 0.0), axis=1, keepdims=True)
-    second_step = jnp.sum(jnp.where(left, 0.0, step_terms), axis=1, keepdims=True)
-    count = WIDTH * lax.broadcasted_iota(jnp.int32, (2, WIDTH), 0) + lax.broadcasted_iota(
-        jnp.int32, (2, WIDTH), 1
-    )
-    line_rows[0:2, :] = jnp.where(
-        count == 2 * me, first_step, jnp.where(count == 2 * me + 1, second_step, 0.0)
-    )
-    part = cross_in.at[pl.ds(0, 3)]
-    pltpu.make_async_copy(part, part, cross_sem).wait()
-    line_rows[2:3, :] = (cross_in[0] + cross_in[1]) + (cross_in[2] + cross_in[3])
-    line_rows[3:4, :] = jnp.zeros_like(step_row)
-    line_in[2 * y + core] = line_rows[...]
-    line = [16 * at_y + 2 * z + at_core for at_y in around_y for at_core in (1 - core, core)]
+    def await_bytes(part, *semaphores):
+        for semaphore in semaphores:
+            pltpu.make_async_copy(part, part, semaphore).wait()
+
+    ends = [16 * at_y + 2 * z + at_core for at_y in around_y for at_core in (1 - core, core)]
     column = [16 * y + 2 * at_z + at_core for at_z in around_z for at_core in (1 - core, core)]
-    for peer in line[:-1]:
-        send(line_rows, line_in.at[2 * y + core], send_sem.at[4], line_sem, {"seq": peer})
-    real_line = readout_out.at[0, :, z, core]
-    imag_line = readout_out.at[1, y, :, core]
-    real_seven = readout_out.at[0, pl.ds(0, 7), 0, 0]
-    pltpu.make_async_copy(real_seven, real_seven, readout_sem.at[0]).wait()
+    real_line = readout_all.at[0, :, z, core]
+    imag_line = readout_all.at[1, y, :, core]
+    seven = readout_all.at[0, pl.ds(0, 7), 0, 0]
+    await_bytes(seven, readout_sem.at[0])
     for peer in column[:-1]:
         send(real_line, real_line, send_sem.at[7], readout_sem.at[2], {"seq": peer})
-    pltpu.make_async_copy(real_seven, real_seven, readout_sem.at[1]).wait()
-    for peer in line[:-1]:
+    await_bytes(seven, readout_sem.at[1])
+    for peer in ends[:-1]:
         send(imag_line, imag_line, send_sem.at[8], readout_sem.at[3], {"seq": peer})
-    part = line_in.at[pl.ds(0, 15)]
-    pltpu.make_async_copy(part, part, line_sem).wait()
-    column_rows[...] = sum_in_order(line_in, 16)
-    column_in[z] = column_rows[...]
-    for at_z in around_z[:-1]:
-        send(
-            column_rows,
-            column_in.at[z],
-            send_sem.at[5],
-            column_sem,
-            {"seq": 16 * y + 2 * at_z + core},
-        )
-    part = column_in.at[pl.ds(0, 7)]
-    pltpu.make_async_copy(part, part, column_sem).wait()
-    sums_out[...] = sum_in_order(column_in, 8)
-
+
+    most = state_in.reshape(32, 1, WIDTH).at[pl.ds(0, 31)]
+    await_bytes(most, state_sem)
+    await_bytes(step_in.at[pl.ds(0, 7)], step_sem)
+    column_rows[0:2, :] = sum_in_order(step_in, 8)
+    column_rows[2:3, :] = sum_rows(state_in.reshape(32, WIDTH)[...])
+    column_rows[3:4, :] = jnp.zeros_like(step_row)
+    column_in[2 * z + core] = column_rows[...]
+    for peer in column[:-1]:
+        send(column_rows, column_in.at[2 * z + core], send_sem.at[5], column_sem, {"seq": peer})
+
+    fifteen = readout_all.at[0].reshape(16, 8, 1, WIDTH).at[pl.ds(0, 15)]
+    await_bytes(fifteen, readout_sem.at[2], readout_sem.at[3])
+    sorted_ = sort_channels(readout_all.reshape(2, OWNERS, WIDTH))
+    sorted_out[0] = sorted_[:STATES]
+    sorted_out[1] = sorted_[STATES:]
     own_lags.wait()
     part = lags_out.at[pl.ds(0, OWNERS - 1)]
-    pltpu.make_async_copy(part, part, lag_sem).wait()
-    pltpu.make_async_copy(part, part, send_sem.at[1]).wait()
-    part = readout_out.at[0].reshape(16, 8, 1, WIDTH).at[pl.ds(0, 15)]
-    pltpu.make_async_copy(part, part, readout_sem.at[2]).wait()
-    pltpu.make_async_copy(part, part, readout_sem.at[3]).wait()
-    pltpu.make_async_copy(part, part, send_sem.at[7]).wait()
-    pltpu.make_async_copy(part, part, send_sem.at[8]).wait()
-    pltpu.make_async_copy(real_seven, real_seven, send_sem.at[2]).wait()
-    pltpu.make_async_copy(real_seven, real_seven, send_sem.at[6]).wait()
-    pltpu.make_async_copy(rest, rest, send_sem.at[0]).wait()
-    for buffer, count_sent, place in ((cross_in, 3, 3), (line_in, 15, 4), (column_in, 7, 5)):
-        part = buffer.at[pl.ds(0, count_sent)]
-        pltpu.make_async_copy(part, part, send_sem.at[place]).wait()
+    await_bytes(part, lag_sem, send_sem.at[1])
+    await_bytes(fifteen, send_sem.at[7], send_sem.at[8])
+    await_bytes(seven, send_sem.at[2], send_sem.at[6])
+    await_bytes(rest, send_sem.at[0])
+    await_bytes(most, send_sem.at[3])
+    await_bytes(step_in.at[pl.ds(0, 7)], send_sem.at[4])
+    ended = column_in.at[pl.ds(0, 15)]
+    await_bytes(ended, column_sem)
+    sums = sum_in_order(column_in, 16)
+    step_out[...] = sums[0:2, :]
+    state_out[0:1, :] = sums[2:3, :STATES]
+    state_out[1:2, :] = sums[2:3, STATES:]
+    await_bytes(ended, send_sem.at[5])
 
 
 def sum_in_order(buffer, count):
@@ -486,30 +498,31 @@
     return parts[0]
 
 
-def finish(
-    lags_ref, readout_ref, sums_ref, lags_out, readout_out, step_out, state_out, lag_sem
-):
-    lags = pltpu.make_async_copy(lags_ref, lags_out, lag_sem)
-    lags.start()
+def sort_channels(rows_ref):
     blocks = []
     for part in range(2):
-        turned = jnp.transpose(readout_ref[part], (1, 0))
+        turned = jnp.transpose(rows_ref[part], (1, 0))
         blocks.append(jnp.concatenate([turned[:STATES], turned[STATES:]], axis=1))
     value = jnp.concatenate(blocks, axis=0)
     at_row = lax.broadcasted_iota(jnp.int32, (2 * OWNERS, 2 * OWNERS), 0)
     at_column = lax.broadcasted_iota(jnp.int32, (2 * OWNERS, 2 * OWNERS), 1)
-    places = 2 * (at_row % OWNERS) + at_row // OWNERS
+    places = jnp.where(at_row < OWNERS, 2 * at_row, 2 * at_row - 2 * OWNERS + 1)
     order = jnp.where(at_column == places, 1.0, 0.0).astype(jnp.bfloat16)
     high = value.astype(jnp.bfloat16)
-    left = value - high.astype(jnp.float32)
-    middle, low = halves(left)
-    sorted_ = dot(high, order) + (dot(middle, order) + dot(low, order))
-    readout_out[0] = sorted_[:STATES]
-    readout_out[1] = sorted_[STATES:]
-    step_out[...] = sums_ref[0:2, :]
-    state_out[0:1, :] = sums_ref[2:3, :STATES]
-    state_out[1:2, :] = sums_ref[2:3, STATES:]
-    lags.wait()
+    middle, low = halves(value - high.astype(jnp.float32))
+    return dot(high, order) + (dot(middle, order) + dot(low, order))
+
+
+def finish(*refs):
+    count = len(refs) // 2
+    copies = [
+        pltpu.make_async_copy(refs[place], refs[count + place], refs[-1].at[place])
+        for place in range(count)
+    ]
+    for copy in copies:
+        copy.start()
+    for copy in copies:
+        copy.wait()
 
 
 def keep(value):
@@ -522,27 +535,29 @@
     any_space = pl.BlockSpec(memory_space=pl.ANY)
     vmem = pl.BlockSpec(memory_space=pltpu.VMEM)
     f32 = jnp.float32
-    lags, readout_rows, sums = pl.pallas_call(
+    results = pl.pallas_call(
         functools.partial(kernel, norm_scale),
         out_shape=(
             pltpu.VMEM((OWNERS, 2, WIDTH), f32),
-            pltpu.VMEM((2, 8, 8, 2, 1, WIDTH), f32),
-            pltpu.VMEM((4, WIDTH), f32),
+            pltpu.VMEM((2, STATES, 2 * OWNERS), f32),
+            pltpu.VMEM((2, WIDTH), f32),
+            pltpu.VMEM((2, STATES), f32),
         ),
         in_specs=[any_space] * 11,
-        out_specs=(vmem, vmem, vmem),
+        out_specs=(vmem,) * 4,
         scratch_shapes=[
             pltpu.VMEM((2, OWNERS, 2, WIDTH), jnp.bfloat16),
             pltpu.VMEM((2, OWNERS, 2, WIDTH), jnp.bfloat16),
             pltpu.VMEM((OWNERS, 2, WIDTH), f32),
             pltpu.VMEM((2, 1, WIDTH), f32),
+            pltpu.VMEM((2, 8, 8, 2, 1, WIDTH), f32),
             pltpu.VMEM((2 * OWNERS, WIDTH), f32),
             pltpu.VMEM((1, WIDTH), f32),
-            pltpu.VMEM((4, 1, WIDTH), f32),
+            pltpu.VMEM((4, 8, 1, WIDTH), f32),
+            pltpu.VMEM((2, WIDTH), f32),
+            pltpu.VMEM((8, 2, WIDTH), f32),
             pltpu.VMEM((4, WIDTH), f32),
             pltpu.VMEM((16, 4, WIDTH), f32),
-            pltpu.VMEM((4, WIDTH), f32),
-            pltpu.VMEM((8, 4, WIDTH), f32),
         ]
         + [
             pltpu.VMEM((2, STATES, 2 * OWNERS), f32),
@@ -571,15 +586,11 @@
             jax.ShapeDtypeStruct((2, WIDTH), f32),
             jax.ShapeDtypeStruct((2, STATES), f32),
         ),
-        in_specs=[vmem] * 3,
-        out_specs=(any_space, vmem, vmem, vmem),
-        scratch_shapes=[dma],
+        in_specs=[vmem] * 4,
+        out_specs=(any_space,) * 4,
+        scratch_shapes=[dma((4,))],
         name="finish",
-    )(
-        keep(lags.reshape(2 * OWNERS, WIDTH)),
-        keep(readout_rows.reshape(2, OWNERS, WIDTH)),
-        keep(sums),
-    )
+    )(*[keep(value) for value in (results[0].reshape(2 * OWNERS, WIDTH), *results[1:])])
     return (
         kernel_grad,
         jnp.transpose(readout_grad, (0, 2, 1)),

time: 41.1 us -> 39.3 us (0.956)
  Pallas kernels: 40.3 us -> 38.5 us
    pallas_call x1, Pallas kernels: 39 us -> 37.8 us  [per_device(): pl.pallas_call(functools.partial(kernel, norm_scale), out_shape=(pltpu.VM...]
    pallas_call x1, Pallas kernels: 1.33 us -> 0.74 us  [per_device(): pl.pallas_call(finish, out_shape=(jax.ShapeDtypeStruct((2 * OWNERS, WIDTH...]
where the time goes in v4:
time: 39.3 us; the launch traced here: 39.2 us
  Pallas kernels  38.5 us (98%)
  between operations  0.64 us (2%)
    pallas_call x1, Pallas kernels, per_device(): pl.pallas_call(functools.partial(kernel, norm_scale), out_shape=(pltpu.VM...  37.8 us

profile of v4, /device:TPU:1, one launch (start us, length us, event | category | flops | bytes accessed | tf_op | source)
XLA Modules:
  0.0 39.2 jit_solution(15146231654300268062)
XLA Ops:
  0.6 37.8 %channel_rows.1 = (f32[128,2,128]{2,1,0:T(2,128)S(1)}, f32[2,64,256]{2,1,0:T(8,128)S(1)}, f32[2,128]{1,0:T(2,128)S(1)}, f32[2,64]{1,0:T(2,128)S(1)}) custom-call(bf16[128,2,128]{2,1,0:T(2,128)(2,1)} %bitcast.10, bf16[128,2,128]{2,1,0:T(2,128)(2,1)} %bitcast.11, f32[2,64,256]{2,1,0:T(8,128)} %bitcast.9, f32[256]{0:T(256)} %log_step_in.1, f32[1,64]{1,0:T(1,128)} %bitcast.12, ...), custom_call_target="tpu_custom_call" | custom-call | tf_op jit(solution)/shard_map/channel_rows/pallas_call | solution.py:538
  38.4 0.7 %finish.1 = (f32[256,128]{1,0:T(8,128)}, f32[2,64,256]{2,1,0:T(8,128)}, f32[2,128]{1,0:T(2,128)}, f32[2,64]{1,0:T(2,128)}) custom-call(f32[256,128]{1,0:T(8,128)S(1)} %bitcast.8, f32[2,64,256]{2,1,0:T(8,128)S(1)} %get-tuple-element.13.refs_1_, f32[2,128]{1,0:T(2,128)S(1)} %get-tuple-element.14.refs_2_, f32[2,64]{1,0:T(2,128)S(1)} %get-tuple-element.15.refs_3_), custom_call_target="tpu_custom_call" | custom-call | tf_op jit(solution)/shard_map/finish/pallas_call | solution.py:581

commit v5 on v4

--- a/solution.py
+++ b/solution.py
@@ -11,6 +11,8 @@
 
 MESH = pl.DeviceIdType.MESH
 OWNERS = 128
+FIRST_ROW = 0
+FIRST = 1
 WIDTH = 128
 LENGTH = OWNERS * WIDTH
 STATES = 64
@@ -264,6 +266,9 @@
     step_in,
     column_rows,
     column_in,
+    column_step_rows,
+    column_step_in,
+    first_in,
     readout_ref,
     log_step_ref,
     decay_ref,
@@ -283,10 +288,14 @@
     state_sem,
     step_sem,
     column_sem,
+    column_step_sem,
+    first_sem,
 ):
     me = lax.axis_index("seq")
     row = lax.axis_index("ch")
     y, z, core = place_of(me)
+    is_first = jnp.logical_and(row == FIRST_ROW, me == FIRST)
+    feeds_first = jnp.logical_and(row == FIRST_ROW, jnp.logical_and(y == 0, me != FIRST))
     stages = [
         pltpu.make_async_copy(inputs_ref, outgoing.at[0], stage_sem.at[0]),
         pltpu.make_async_copy(grads_ref, outgoing.at[1], stage_sem.at[1]),
@@ -307,6 +316,19 @@
         pl.semaphore_signal(
             barrier, inc=1, device_id={"ch": at_x, "seq": peer}, device_id_type=MESH
         )
+
+    @pl.when(is_first)
+    def _():
+        for at_x in around_x[:3]:
+
+            def hail(peer, carry, at_x=at_x):
+                pl.semaphore_signal(
+                    barrier, inc=1, device_id={"ch": at_x, "seq": peer}, device_id_type=MESH
+                )
+                return carry
+
+            lax.fori_loop(0, OWNERS, hail, 0)
+
     loads = [
         pltpu.make_async_copy(source, target, table_sem.at[place])
         for place, (source, target) in enumerate(
@@ -327,7 +349,7 @@
         copy.start()
     for copy in stages:
         copy.wait()
-    pl.semaphore_wait(barrier, OWNERS - 1 + len(across))
+    pl.semaphore_wait(barrier, OWNERS - 1 + len(across) + (row + 3) // 4)
 
     def send(source, target, sent, received, device):
         pltpu.make_async_remote_copy(
@@ -394,6 +416,17 @@
         state_grad[1] + pltpu.roll(state_grad[1], STATES, 1),
     )
     line = [16 * at_y + 2 * z + core for at_y in around_y[:-1]]
+
+    @pl.when(jnp.logical_not(is_first))
+    def _():
+        send(
+            state_rows,
+            first_in.at[2 * z + core, 8 * row + y],
+            send_sem.at[9],
+            first_sem,
+            {"ch": jnp.int32(FIRST_ROW), "seq": jnp.int32(FIRST)},
+        )
+
     for at_x, peer in across + [(around_x[3], peer) for peer in line]:
         send(
             state_rows,
@@ -403,6 +436,11 @@
             {"ch": at_x, "seq": peer},
         )
     state_in[row, y] = state_rows[...]
+
+    @pl.when(is_first)
+    def _():
+        first_in[FIRST, 0] = state_rows[...]
+
     first_step = jnp.sum(jnp.where(left, step_terms, 0.0), axis=1, keepdims=True)
     second_step = jnp.sum(jnp.where(left, 0.0, step_terms), axis=1, keepdims=True)
     count = WIDTH * lax.broadcasted_iota(jnp.int32, (2, WIDTH), 0) + lax.broadcasted_iota(
@@ -460,14 +498,27 @@
         send(imag_line, imag_line, send_sem.at[8], readout_sem.at[3], {"seq": peer})
 
     most = state_in.reshape(32, 1, WIDTH).at[pl.ds(0, 31)]
+    await_bytes(step_in.at[pl.ds(0, 7)], step_sem)
+    column_step_rows[...] = sum_in_order(step_in, 8)
+    column_step_in[2 * z + core] = column_step_rows[...]
+    for peer in column[:-1]:
+        send(
+            column_step_rows,
+            column_step_in.at[2 * z + core],
+            send_sem.at[10],
+            column_step_sem,
+            {"seq": peer},
+        )
     await_bytes(most, state_sem)
-    await_bytes(step_in.at[pl.ds(0, 7)], step_sem)
-    column_rows[0:2, :] = sum_in_order(step_in, 8)
-    column_rows[2:3, :] = sum_rows(state_in.reshape(32, WIDTH)[...])
-    column_rows[3:4, :] = jnp.zeros_like(step_row)
+    column_rows[...] = sum_rows(state_in.reshape(32, WIDTH)[...])
     column_in[2 * z + core] = column_rows[...]
     for peer in column[:-1]:
-        send(column_rows, column_in.at[2 * z + core], send_sem.at[5], column_sem, {"seq": peer})
+
+        @pl.when(jnp.logical_or(row != FIRST_ROW, peer != FIRST))
+        def _(peer=peer):
+            send(
+                column_rows, column_in.at[2 * z + core], send_sem.at[5], column_sem, {"seq": peer}
+            )
 
     fifteen = readout_all.at[0].reshape(16, 8, 1, WIDTH).at[pl.ds(0, 15)]
     await_bytes(fifteen, readout_sem.at[2], readout_sem.at[3])
@@ -482,13 +533,30 @@
     await_bytes(rest, send_sem.at[0])
     await_bytes(most, send_sem.at[3])
     await_bytes(step_in.at[pl.ds(0, 7)], send_sem.at[4])
-    ended = column_in.at[pl.ds(0, 15)]
-    await_bytes(ended, column_sem)
-    sums = sum_in_order(column_in, 16)
-    step_out[...] = sums[0:2, :]
-    state_out[0:1, :] = sums[2:3, :STATES]
-    state_out[1:2, :] = sums[2:3, STATES:]
-    await_bytes(ended, send_sem.at[5])
+    step_ended = column_step_in.at[pl.ds(0, 15)]
+    await_bytes(step_ended, column_step_sem, send_sem.at[10])
+    step_out[...] = sum_in_order(column_step_in, 16)
+    await_bytes(column_in.at[pl.ds(0, 14)], send_sem.at[5])
+
+    def put_state(state):
+        state_out[0:1, :] = state[:, :STATES]
+        state_out[1:2, :] = state[:, STATES:]
+
+    @pl.when(jnp.logical_not(feeds_first))
+    def _():
+        await_bytes(column_in.at[pl.ds(0, 1)], send_sem.at[5])
+
+    @pl.when(is_first)
+    def _():
+        await_bytes(first_in.reshape(512, 1, WIDTH).at[pl.ds(0, 511)], first_sem)
+        every = first_in.reshape(16, 32, WIDTH)
+        put_state(sum_in_order([sum_rows(every[place]) for place in range(16)], 16))
+
+    @pl.when(jnp.logical_not(is_first))
+    def _():
+        await_bytes(column_in.at[pl.ds(0, 1)], send_sem.at[9])
+        await_bytes(column_in.at[pl.ds(0, 15)], column_sem)
+        put_state(sum_in_order(column_in, 16))
 
 
 def sum_in_order(buffer, count):
@@ -556,8 +624,11 @@
             pltpu.VMEM((4, 8, 1, WIDTH), f32),
             pltpu.VMEM((2, WIDTH), f32),
             pltpu.VMEM((8, 2, WIDTH), f32),
-            pltpu.VMEM((4, WIDTH), f32),
-            pltpu.VMEM((16, 4, WIDTH), f32),
+            pltpu.VMEM((1, WIDTH), f32),
+            pltpu.VMEM((16, 1, WIDTH), f32),
+            pltpu.VMEM((2, WIDTH), f32),
+            pltpu.VMEM((16, 2, WIDTH), f32),
+            pltpu.VMEM((16, 32, 1, WIDTH), f32),
         ]
         + [
             pltpu.VMEM((2, STATES, 2 * OWNERS), f32),
@@ -566,7 +637,7 @@
             pltpu.VMEM((1, STATES), f32),
         ]
         + [pltpu.VMEM(table.shape, table.dtype) for table in tables]
-        + [dma((2,)), dma((9,)), dma((2,)), dma((9,)), dma, dma, dma((4,)), dma, dma, dma],
+        + [dma((2,)), dma((9,)), dma((2,)), dma((11,)), dma, dma, dma((4,)), dma, dma, dma, dma, dma],
         compiler_params=pltpu.CompilerParams(collective_id=0, has_side_effects=True),
         name="channel_rows",
     )(

time: 39.3 us -> 39.4 us (level)
  no operation moved by 1% of the time
where the time goes in v5:
time: 39.4 us; the launch traced here: 39.3 us
  Pallas kernels  38.6 us (98%)
  between operations  0.64 us (2%)
    pallas_call x1, Pallas kernels, per_device(): pl.pallas_call(functools.partial(kernel, norm_scale), out_shape=(pltpu.VM...  37.9 us

profile of v5, /device:TPU:1, one launch (start us, length us, event | category | flops | bytes accessed | tf_op | source)
XLA Modules:
  0.0 39.3 jit_solution(13047159134957414388)
XLA Ops:
  0.6 37.9 %channel_rows.1 = (f32[128,2,128]{2,1,0:T(2,128)S(1)}, f32[2,64,256]{2,1,0:T(8,128)S(1)}, f32[2,128]{1,0:T(2,128)S(1)}, f32[2,64]{1,0:T(2,128)S(1)}) custom-call(bf16[128,2,128]{2,1,0:T(2,128)(2,1)} %bitcast.10, bf16[128,2,128]{2,1,0:T(2,128)(2,1)} %bitcast.11, f32[2,64,256]{2,1,0:T(8,128)} %bitcast.9, f32[256]{0:T(256)} %log_step_in.1, f32[1,64]{1,0:T(1,128)} %bitcast.12, ...), custom_call_target="tpu_custom_call" | custom-call | tf_op jit(solution)/shard_map/channel_rows/pallas_call | solution.py:606
  38.5 0.7 %finish.1 = (f32[256,128]{1,0:T(8,128)}, f32[2,64,256]{2,1,0:T(8,128)}, f32[2,128]{1,0:T(2,128)}, f32[2,64]{1,0:T(2,128)}) custom-call(f32[256,128]{1,0:T(8,128)S(1)} %bitcast.8, f32[2,64,256]{2,1,0:T(8,128)S(1)} %get-tuple-element.13.refs_1_, f32[2,128]{1,0:T(2,128)S(1)} %get-tuple-element.14.refs_2_, f32[2,64]{1,0:T(2,128)S(1)} %get-tuple-element.15.refs_3_), custom_call_target="tpu_custom_call" | custom-call | tf_op jit(solution)/shard_map/finish/pallas_call | solution.py:652

commit v6 on v4

--- a/solution.py
+++ b/solution.py
@@ -225,14 +225,21 @@
     return [(place + offset_of(count, ring)) % ring for count in range(ring)]
 
 
+def hop_order():
+    draws = np.random.RandomState(0).permutation(OWNERS)
+    offsets = [(at // 16, at // 2 % 8, at % 2) for at in range(1, OWNERS)]
+    hops = [min(y, 8 - y) + min(z, 8 - z) for y, z, _ in offsets]
+    places = sorted(range(OWNERS - 1), key=lambda at: (-hops[at], draws[at]))
+    return [offsets[at] for at in places]
+
+
 def per_peer(me, action):
     y, z, core = place_of(me)
-    to_y = [16 * other for other in ring_places(y, 8)]
-    to_z = [2 * other for other in ring_places(z, 8)]
-    to_core = [1 - core, core]
-    peers = [at_y + at_z + at_core for at_y in to_y for at_z in to_z for at_core in to_core]
-    for peer in peers[:-1]:
-        action(peer)
+    to_y = [16 * ((y + step) % 8) for step in range(8)]
+    to_z = [2 * ((z + step) % 8) for step in range(8)]
+    to_core = [core, 1 - core]
+    for step_y, step_z, step_core in hop_order():
+        action(to_y[step_y] + to_z[step_z] + to_core[step_core])
 
 
 def kernel(

time: 39.3 us -> 38.8 us (0.987)
  Pallas kernels: 38.5 us -> 38.1 us
    pallas_call x1, Pallas kernels: 37.8 us -> 37.3 us  [per_device(): pl.pallas_call(functools.partial(kernel, norm_scale), out_shape=(pltpu.VM...]
where the time goes in v6:
time: 38.8 us; the launch traced here: 38.7 us
  Pallas kernels  38.1 us (98%)
  between operations  0.64 us (2%)
    pallas_call x1, Pallas kernels, per_device(): pl.pallas_call(functools.partial(kernel, norm_scale), out_shape=(pltpu.VM...  37.3 us

profile of v6, /device:TPU:1, one launch (start us, length us, event | category | flops | bytes accessed | tf_op | source)
XLA Modules:
  0.0 38.7 jit_solution(6288489098362031163)
XLA Ops:
  0.6 37.3 %channel_rows.1 = (f32[128,2,128]{2,1,0:T(2,128)S(1)}, f32[2,64,256]{2,1,0:T(8,128)S(1)}, f32[2,128]{1,0:T(2,128)S(1)}, f32[2,64]{1,0:T(2,128)S(1)}) custom-call(bf16[128,2,128]{2,1,0:T(2,128)(2,1)} %bitcast.10, bf16[128,2,128]{2,1,0:T(2,128)(2,1)} %bitcast.11, f32[2,64,256]{2,1,0:T(8,128)} %bitcast.9, f32[256]{0:T(256)} %log_step_in.1, f32[1,64]{1,0:T(1,128)} %bitcast.12, ...), custom_call_target="tpu_custom_call" | custom-call | tf_op jit(solution)/shard_map/channel_rows/pallas_call | solution.py:545
  38.0 0.7 %finish.1 = (f32[256,128]{1,0:T(8,128)}, f32[2,64,256]{2,1,0:T(8,128)}, f32[2,128]{1,0:T(2,128)}, f32[2,64]{1,0:T(2,128)}) custom-call(f32[256,128]{1,0:T(8,128)S(1)} %bitcast.8, f32[2,64,256]{2,1,0:T(8,128)S(1)} %get-tuple-element.13.refs_1_, f32[2,128]{1,0:T(2,128)S(1)} %get-tuple-element.14.refs_2_, f32[2,64]{1,0:T(2,128)S(1)} %get-tuple-element.15.refs_3_), custom_call_target="tpu_custom_call" | custom-call | tf_op jit(solution)/shard_map/finish/pallas_call | solution.py:588

commit v7 on v6

--- a/solution.py
+++ b/solution.py
@@ -271,6 +271,7 @@
     step_in,
     column_rows,
     column_in,
+    order,
     readout_ref,
     log_step_ref,
     decay_ref,
@@ -382,6 +383,7 @@
     for copy in loads[4:]:
         copy.wait()
 
+    order[...] = channel_order()
     own.wait()
     rest = arrived.at[:, pl.ds(0, OWNERS - 1)]
     pltpu.make_async_copy(rest, rest, signal_sem).wait()
@@ -477,10 +479,10 @@
         send(column_rows, column_in.at[2 * z + core], send_sem.at[5], column_sem, {"seq": peer})
 
     fifteen = readout_all.at[0].reshape(16, 8, 1, WIDTH).at[pl.ds(0, 15)]
-    await_bytes(fifteen, readout_sem.at[2], readout_sem.at[3])
-    sorted_ = sort_channels(readout_all.reshape(2, OWNERS, WIDTH))
-    sorted_out[0] = sorted_[:STATES]
-    sorted_out[1] = sorted_[STATES:]
+    rows = readout_all.reshape(2, OWNERS, WIDTH)
+    for part in range(2):
+        await_bytes(fifteen, readout_sem.at[2 + part])
+        sorted_out[part] = sort_channels(rows[part], order[...])
     own_lags.wait()
     part = lags_out.at[pl.ds(0, OWNERS - 1)]
     await_bytes(part, lag_sem, send_sem.at[1])
@@ -505,16 +507,16 @@
     return parts[0]
 
 
-def sort_channels(rows_ref):
-    blocks = []
-    for part in range(2):
-        turned = jnp.transpose(rows_ref[part], (1, 0))
-        blocks.append(jnp.concatenate([turned[:STATES], turned[STATES:]], axis=1))
-    value = jnp.concatenate(blocks, axis=0)
+def channel_order():
     at_row = lax.broadcasted_iota(jnp.int32, (2 * OWNERS, 2 * OWNERS), 0)
     at_column = lax.broadcasted_iota(jnp.int32, (2 * OWNERS, 2 * OWNERS), 1)
     places = jnp.where(at_row < OWNERS, 2 * at_row, 2 * at_row - 2 * OWNERS + 1)
-    order = jnp.where(at_column == places, 1.0, 0.0).astype(jnp.bfloat16)
+    return jnp.where(at_column == places, 1.0, 0.0).astype(jnp.bfloat16)
+
+
+def sort_channels(rows, order):
+    turned = jnp.transpose(rows, (1, 0))
+    value = jnp.concatenate([turned[:STATES], turned[STATES:]], axis=1)
     high = value.astype(jnp.bfloat16)
     middle, low = halves(value - high.astype(jnp.float32))
     return dot(high, order) + (dot(middle, order) + dot(low, order))
@@ -565,6 +567,7 @@
             pltpu.VMEM((8, 2, WIDTH), f32),
             pltpu.VMEM((4, WIDTH), f32),
             pltpu.VMEM((16, 4, WIDTH), f32),
+            pltpu.VMEM((2 * OWNERS, 2 * OWNERS), jnp.bfloat16),
         ]
         + [
             pltpu.VMEM((2, STATES, 2 * OWNERS), f32),

time: 38.8 us -> 38.8 us (level)
  no operation moved by 1% of the time
where the time goes in v7:
time: 38.8 us; the launch traced here: 38.7 us
  Pallas kernels  38.1 us (98%)
  between operations  0.64 us (2%)
    pallas_call x1, Pallas kernels, per_device(): pl.pallas_call(functools.partial(kernel, norm_scale), out_shape=(pltpu.VM...  37.3 us

profile of v7, /device:TPU:1, one launch (start us, length us, event | category | flops | bytes accessed | tf_op | source)
XLA Modules:
  0.0 38.7 jit_solution(17905152444965984497)
XLA Ops:
  0.6 37.3 %channel_rows.1 = (f32[128,2,128]{2,1,0:T(2,128)S(1)}, f32[2,64,256]{2,1,0:T(8,128)S(1)}, f32[2,128]{1,0:T(2,128)S(1)}, f32[2,64]{1,0:T(2,128)S(1)}) custom-call(bf16[128,2,128]{2,1,0:T(2,128)(2,1)} %bitcast.10, bf16[128,2,128]{2,1,0:T(2,128)(2,1)} %bitcast.11, f32[2,64,256]{2,1,0:T(8,128)} %bitcast.9, f32[256]{0:T(256)} %log_step_in.1, f32[1,64]{1,0:T(1,128)} %bitcast.12, ...), custom_call_target="tpu_custom_call" | custom-call | tf_op jit(solution)/shard_map/channel_rows/pallas_call | solution.py:547
  38.0 0.7 %finish.1 = (f32[256,128]{1,0:T(8,128)}, f32[2,64,256]{2,1,0:T(8,128)}, f32[2,128]{1,0:T(2,128)}, f32[2,64]{1,0:T(2,128)}) custom-call(f32[256,128]{1,0:T(8,128)S(1)} %bitcast.8, f32[2,64,256]{2,1,0:T(8,128)S(1)} %get-tuple-element.13.refs_1_, f32[2,128]{1,0:T(2,128)S(1)} %get-tuple-element.14.refs_2_, f32[2,64]{1,0:T(2,128)S(1)} %get-tuple-element.15.refs_3_), custom_call_target="tpu_custom_call" | custom-call | tf_op jit(solution)/shard_map/finish/pallas_call | solution.py:591
